TPU v7x, 128 devices: a whole 4x4x4 slice. The times are simulated.
128 devices in a mesh: sec: 2 (over core), dev: 64 (over z, x, y).
Axes of the slice: x: 4, y: 4, z: 4, core: 2. Of those that a mesh axis runs over, the one named last changes fastest.
Arguments:
- tokens: bfloat16 [2048, 3584], P(('sec', 'dev')), may hold values from -6 to 6
- routes: int32 [2048, 8], P(('sec', 'dev')), may hold values from 0 to 127, all different within a row; in each aligned block of 16 rows (0 to 15, 16 to 31, ...) at most 2 rows name the same one
- gate_num: int32 [2048, 8], P(('sec', 'dev')), may hold values from 1 to 32
- w_gate: bfloat16 [128, 3584, 1024], P(('sec', 'dev')), may hold values from -0.09375 to 0.09375
- w_up: bfloat16 [128, 3584, 1024], P(('sec', 'dev')), may hold values from -0.09375 to 0.09375
- w_down: bfloat16 [128, 1024, 3584], P(('sec', 'dev')), may hold values from -0.1875 to 0.1875
- attn_gain: float32 [3584], replicated, may hold values from 0.25 to 1.75
- w_latent: bfloat16 [3584, 576], P('dev'), may hold values from -0.09375 to 0.09375
- kv_gain: float32 [512], replicated, may hold values from 0.25 to 1.75
- queries: bfloat16 [2048, 64, 576], P(('sec', 'dev')), may hold values from -9 to 9
- cache_pool: bfloat16 [4096, 64, 576], P(('sec', 'dev')), may hold values from -4 to 4
- block_table: int32 [2048, 4], P(('sec', 'dev')), may hold values from 0 to 31
- lengths: int32 [128, 16], P(('sec', 'dev')), may hold values from 1 to 256, 2048 in all within a row
Outputs:
- layer_out: bfloat16 [2048, 3584], P(('sec', 'dev'))
- new_latent: bfloat16 [2048, 576], P(('sec', 'dev'))
- context: bfloat16 [2048, 32768], P(('sec', 'dev'))
Inputs may be any that keep to these rules, and one draw needn't show every extreme that they name: `routes`: in each aligned block of 16 rows (the rows of one device) no expert is named by more than 2 rows. `block_table`: each device's rows point only into that device's 32 pages; pages may be shared by rows. The 16 lengths of one device add up to 2048.
All inputs are finite; a program needn't handle non-finite values.
Results may differ from a plain program's by a relative error of at most 0.0064.
Values may be sent and summed in bfloat16 or wider, within the bound.
A program may use at most 128 MiB of HBM per device.

v0:
```python
import jax
import jax.numpy as jnp
from jax import lax
from jax.sharding import PartitionSpec as P

GATE_DEN = 32


score_scale = 192.0 ** (-0.5)
norm_eps = 1e-06


def slot_numbers(expert_rows, expert_count):
    onehot = (expert_rows[:, None] == jnp.arange(expert_count, dtype=jnp.int32)[None, :]).astype(
        jnp.int32
    )
    before = jnp.cumsum(onehot, axis=0) - onehot
    return jnp.sum(before * onehot, axis=1)


def rms_scale(values, gain):
    mean_square = jnp.mean(values * values, axis=-1, keepdims=True)
    return values * lax.rsqrt(mean_square + norm_eps) * gain


def expert_apply(rows, gates, gate_proj, up_proj, down_proj):
    gate_part = jnp.dot(rows, gate_proj, preferred_element_type=jnp.float32)
    up_part = jnp.dot(rows, up_proj, preferred_element_type=jnp.float32)
    hidden = (jax.nn.silu(gate_part) * up_part).astype(jnp.bfloat16)
    result = jnp.dot(hidden, down_proj, preferred_element_type=jnp.float32)
    return (result * gates.astype(jnp.float32)[:, None]).astype(jnp.bfloat16)


def per_device(
    tokens,
    routes,
    gate_num,
    w_gate,
    w_up,
    w_down,
    attn_gain,
    w_latent,
    kv_gain,
    queries,
    cache_pool,
    block_table,
    lengths,
):
    sections = lax.axis_size("sec")
    chip_count = lax.axis_size("dev")
    expert_count = sections * chip_count
    tok_rows, width = tokens.shape
    fanout = routes.shape[1]
    expert_rows = routes.reshape(-1)
    row_count = expert_rows.shape[0]
    capacity = 2 * row_count // expert_count
    slots = slot_numbers(expert_rows, expert_count)
    position = expert_rows * capacity + slots
    filled = (
        jnp.zeros((expert_count * capacity,), jnp.int32)
        .at[position]
        .set(jnp.arange(row_count, dtype=jnp.int32) + 1)
    )
    live_slot = filled > 0
    source_row = jnp.maximum(filled - 1, 0)
    send_rows = jnp.where(
        live_slot[:, None], tokens[source_row // fanout], jnp.zeros((), jnp.bfloat16)
    )
    send_rows = send_rows.reshape(expert_count, capacity, width)
    gate_values = gate_num.reshape(-1)[source_row].astype(jnp.float32) / GATE_DEN
    send_gate = (
        jnp.where(live_slot, gate_values, 0.0).astype(jnp.bfloat16).reshape(expert_count, capacity)
    )
    gate_proj, up_proj, down_proj = (w_gate[0], w_up[0], w_down[0])
    rows = lax.all_to_all(send_rows, ("sec", "dev"), split_axis=0, concat_axis=0, tiled=True)
    served = expert_apply(
        rows.reshape(-1, width),
        lax.all_to_all(send_gate, ("sec", "dev"), split_axis=0, concat_axis=0, tiled=True).reshape(
            -1
        ),
        gate_proj,
        up_proj,
        down_proj,
    )
    served = served.reshape(rows.shape)
    returned = lax.all_to_all(served, ("sec", "dev"), split_axis=0, concat_axis=0, tiled=True)
    picked = returned.reshape(expert_count * capacity, width)[position]
    moe = jnp.sum(picked.astype(jnp.float32).reshape(tok_rows, fanout, width), axis=1)
    layer_out = (tokens.astype(jnp.float32) + moe).astype(jnp.bfloat16)
    normed = rms_scale(layer_out.astype(jnp.float32), attn_gain).astype(jnp.bfloat16)
    kdim = w_latent.shape[1]
    lat_width = kv_gain.shape[0]
    latent_full = jnp.dot(
        normed,
        lax.all_gather(w_latent, "dev", axis=0, tiled=True),
        preferred_element_type=jnp.float32,
    )
    latent = rms_scale(latent_full[:, :lat_width], kv_gain)
    new_latent = jnp.concatenate([latent, latent_full[:, lat_width:]], axis=1).astype(jnp.bfloat16)
    page_rows = cache_pool[block_table]
    key_rows = jnp.concatenate(
        [page_rows.reshape(tok_rows, -1, kdim), new_latent[:, None, :]], axis=1
    )
    span = key_rows.shape[1] - 1
    row_lengths = lengths.reshape(-1)
    kept = jnp.concatenate(
        [
            jnp.arange(span, dtype=jnp.int32)[None, :] < row_lengths[:, None],
            jnp.ones((tok_rows, 1), dtype=bool),
        ],
        axis=1,
    )
    scores = (
        jnp.einsum("thk,tpk->thp", queries, key_rows, preferred_element_type=jnp.float32)
        * score_scale
    )
    scores = jnp.where(kept[:, None, :], scores, -1e30)
    top_score = jnp.max(scores, axis=2, keepdims=True)
    raised = jnp.exp(scores - top_score)
    probs = (raised / jnp.sum(raised, axis=2, keepdims=True)).astype(jnp.bfloat16)
    mixed = jnp.einsum(
        "thp,tpl->thl", probs, key_rows[:, :, :lat_width], preferred_element_type=jnp.float32
    )
    context = mixed.astype(jnp.bfloat16).reshape(tok_rows, -1)
    return (layer_out, new_latent, context)


def solution(mesh):
    return jax.shard_map(
        per_device,
        mesh=mesh,
        in_specs=(
            P(("sec", "dev"), None),
            P(("sec", "dev"), None),
            P(("sec", "dev"), None),
            P(("sec", "dev"), None, None),
            P(("sec", "dev"), None, None),
            P(("sec", "dev"), None, None),
            P(),
            P("dev", None),
            P(),
            P(("sec", "dev"), None, None),
            P(("sec", "dev"), None, None),
            P(("sec", "dev"), None),
            P(("sec", "dev"), None),
        ),
        out_specs=(P(("sec", "dev"), None), P(("sec", "dev"), None), P(("sec", "dev"), None)),
        check_vma=False,
    )
```

profile of v0, /device:TPU:0, one launch (start us, length us, event | category | flops | bytes accessed | tf_op | source)
XLA Modules:
  0.0 172.9 jit_solution(1942545158740195579)
XLA Ops:
  7.2 0.0 all-gather.2.cloned.1.call-start
  7.2 0.7 all-gather.2.cloned.1.call-update
  7.9 0.8 broadcast_multiply_fusion
  8.7 0.8 copy.27
  9.5 0.1 eq.15
  9.5 0.1 fusion.48
  9.7 0.8 copy.28
  10.4 0.1 reshape.133
  10.5 0.1 copy.26
  10.6 0.1 mul.81
  10.7 0.2 reduce_window_sum.11
  10.8 0.2 select_reduce_fusion
  11.0 1.0 scatter_custom_fusion
  12.1 1.9 %gather_fusion.1 = s32[256]{0:T(256)S(1)} fusion(s32[128]{0:T(128)S(1)} %reshape.133, s32[1024]{0:T(1024)S(1)} %get-tuple-element.9), kind=kCustom, calls=%fused_computation.1 | custom fusion | bytes 3072 | tf_op jit(solution)/shard_map/gather | solution.py:70
  13.9 0.8 all_to_all.16
  14.7 11.1 %all-to-all-start.1 = ((bf16[128,1,2]{2,1,0:T(2,128)(2,1)}), bf16[128,1,2]{2,1,0:T(2,128)(2,1)S(1)}, u32[]{:S(2)}, u32[]{:S(2)}) async-start(bf16[128,1,2]{2,1,0:T(2,128)(2,1)} %all_to_all.16), calls=%async_computation.1 | async-start | bytes 131072 | tf_op jit(solution)/shard_map/all_to_all | solution.py:78
  25.9 3.0 %gather_fusion = bf16[256,3584]{1,0:T(8,128)(2,1)} fusion(bf16[16,3584]{1,0:T(8,128)(2,1)S(1)} %copy-done.1, s32[1024]{0:T(1024)S(1)} %get-tuple-element.10), kind=kCustom, calls=%fused_computation | custom fusion | bytes 3671040 | tf_op jit(solution)/shard_map/gather | solution.py:67
  28.9 4.8 %gather.15 = bf16[128,2,3584]{2,1,0:T(2,128)(2,1)} reshape(bf16[256,3584]{1,0:T(8,128)(2,1)} %gather_fusion) | data formatting | bytes 3670016 | tf_op jit(solution)/shard_map/gather | solution.py:67
  33.6 0.2 broadcast_in_dim.53
  33.8 4.5 %broadcast_select_fusion = bf16[128,2,3584]{2,1,0:T(2,128)(2,1)} fusion(bf16[128,2,3584]{2,1,0:T(2,128)(2,1)} %gather.15, pred[128,2]{1,0:T(8,128)(4,1)S(1)} %broadcast_in_dim.53), kind=kLoop, calls=%fused_computation.22 | loop fusion | flops 917504 | bytes 3670272 | tf_op jit(solution)/shard_map/jit(_where)/select_n | solution.py:66
  38.3 10.4 %all-to-all-start = ((bf16[128,2,3584]{2,1,0:T(2,128)(2,1)}), bf16[128,2,3584]{2,1,0:T(2,128)(2,1)}, u32[]{:S(2)}, u32[]{:S(2)}) async-start(bf16[128,2,3584]{2,1,0:T(2,128)(2,1)} %broadcast_select_fusion), calls=%async_computation | async-start | bytes 3670016 | tf_op jit(solution)/shard_map/all_to_all | solution.py:75
  48.7 0.2 convert_reduce_fusion.1
  48.9 0.1 reshape.138
  49.0 26.4 %all-to-all-done = bf16[128,2,3584]{2,1,0:T(2,128)(2,1)} async-done(((bf16[128,2,3584]{2,1,0:T(2,128)(2,1)}), bf16[128,2,3584]{2,1,0:T(2,128)(2,1)}, u32[]{:S(2)}, u32[]{:S(2)}) %all-to-all-start) | async-done | bytes 1835040 | tf_op jit(solution)/shard_map/all_to_all | solution.py:75
  75.4 4.9 %reshape.132 = bf16[256,3584]{1,0:T(8,128)(2,1)} reshape(bf16[128,2,3584]{2,1,0:T(2,128)(2,1)} %all-to-all-done) | data formatting | bytes 3670016 | tf_op jit(solution)/shard_map/reshape | solution.py:77
  80.3 7.1 %fusion.5 = f32[256,1024]{1,0:T(8,128)} fusion(bf16[256,3584]{1,0:T(8,128)(2,1)} %reshape.132, bf16[1,3584,1024]{2,1,0:T(8,128)(2,1)} %param.16), kind=kOutput, calls=%fused_computation.10 | convolution fusion | flops 1879048192 | bytes 10223616 | tf_op jit(solution)/shard_map/dot_general | solution.py:27
  87.4 11.6 %fusion.14 = bf16[256,3584]{1,0:T(8,128)(2,1)} fusion(bf16[1,1024,3584]{2,1,0:T(8,128)(2,1)} %param.18, f32[256]{0:T(256)S(1)} %reshape.138, bf16[256,3584]{1,0:T(8,128)(2,1)} %reshape.132, bf16[1,3584,1024]{2,1,0:T(8,128)(2,1)} %param.17, f32[256,1024]{1,0:T(8,128)} %fusion.5), kind=kOutput, calls=%fused_computation.17 | convolution fusion | flops 3761504256 | bytes 19399680 | tf_op jit(solution)/shard_map/dot_general | solution.py:30
  99.0 4.8 %reshape.134 = bf16[128,2,3584]{2,1,0:T(2,128)(2,1)} reshape(bf16[256,3584]{1,0:T(8,128)(2,1)} %fusion.14) | data formatting | bytes 3670016 | tf_op jit(solution)/shard_map/reshape | solution.py:85
  103.8 6.6 %all-to-all-start.2 = ((bf16[128,2,3584]{2,1,0:T(2,128)(2,1)}), bf16[128,2,3584]{2,1,0:T(2,128)(2,1)}, u32[]{:S(2)}, u32[]{:S(2)}) async-start(bf16[128,2,3584]{2,1,0:T(2,128)(2,1)} %reshape.134), calls=%async_computation.2 | async-start | bytes 3670016 | tf_op jit(solution)/shard_map/all_to_all | solution.py:86
  110.5 0.1 copy.30
  110.6 0.1 reshape.166
  110.7 3.5 %gather_fusion.3 = bf16[64,64,576]{2,1,0:T(8,128)(2,1)} fusion(bf16[32,64,576]{2,1,0:T(8,128)(2,1)S(1)} %copy-done, s32[1024]{0:T(1024)S(1)} %pad_clamp_fusion), kind=kCustom, calls=%fused_computation.3 | custom fusion | bytes 9437440 | tf_op jit(solution)/shard_map/gather | solution.py:100
  114.2 0.1 iota_compare_fusion.1
  114.3 21.2 %all-to-all-done.2 = bf16[128,2,3584]{2,1,0:T(2,128)(2,1)} async-done(((bf16[128,2,3584]{2,1,0:T(2,128)(2,1)}), bf16[128,2,3584]{2,1,0:T(2,128)(2,1)}, u32[]{:S(2)}, u32[]{:S(2)}) %all-to-all-start.2) | async-done | bytes 1835040 | tf_op jit(solution)/shard_map/all_to_all | solution.py:86
  135.5 5.0 %reshape.135 = bf16[256,3584]{1,0:T(8,128)(2,1)} reshape(bf16[128,2,3584]{2,1,0:T(2,128)(2,1)} %all-to-all-done.2) | data formatting | bytes 3670016 | tf_op jit(solution)/shard_map/reshape | solution.py:87
  140.5 4.7 %gather_fusion.2 = bf16[128,3584]{1,0:T(8,128)(2,1)} fusion(bf16[256,3584]{1,0:T(8,128)(2,1)} %reshape.135, s32[1024]{0:T(1024)S(1)} %pad_clamp_fusion.1), kind=kCustom, calls=%fused_computation.2 | custom fusion | bytes 1835520 | tf_op jit(solution)/shard_map/gather | solution.py:87
  145.2 1.8 %convert_reduce_fusion = f32[16,3584]{1,0:T(8,128)S(1)} fusion(bf16[128,3584]{1,0:T(8,128)(2,1)} %gather_fusion.2), kind=kLoop, calls=%fused_computation.23 | loop fusion | flops 860160 | bytes 1146880 | tf_op jit(solution)/shard_map/reduce_sum | solution.py:88
  146.9 0.2 fusion.41
  147.2 3.1 %fusion.44 = f32[16,576]{1,0:T(8,128)S(1)} fusion(bf16[3584,576]{1,0:T(8,128)(2,1)} %all-gather.2.cloned.1.call-done, bf16[16,3584]{1,0:T(8,128)(2,1)S(1)} %get-tuple-element.4, f32[3584]{0:T(1024)S(1)} %copy-done.4, f32[16]{0:T(128)S(1)} %add_rsqrt_fusion.1), kind=kOutput, calls=%fused_computation.41 | convolution fusion | flops 66289664 | bytes 4294720 | tf_op jit(solution)/shard_map/dot_general | solution.py:93
  150.3 0.1 multiply_reduce_fusion
  150.5 0.1 multiply_convert_fusion
  150.6 0.1 fusion.65
  150.7 4.6 %multiply_select_fusion = f32[16,257,64]{1,2,0:T(8,128)S(1)} fusion(bf16[16,64,576]{2,1,0:T(8,128)(2,1)S(1)} %copy-done.8, bf16[16,1,576]{2,1,0:T(2,128)(2,1)S(1)} %copy.31, bf16[16,256,576]{2,1,0:T(8,128)(2,1)} %bitcast.52, pred[16,257]{1,0:T(8,128)(4,1)S(1)} %concatenate.25), kind=kOutput, calls=%fused_computation.28 | convolution fusion | flops 313169920 | bytes 6973456 | tf_op jit(solution)/shard_map/thk,tpk->thp/dot_general | solution.py:114
  155.3 1.2 copy-done.2
  156.5 0.5 fusion.60
  156.9 5.8 %fusion.26 = bf16[16,64,512]{2,1,0:T(8,128)(2,1)} fusion(bf16[16,1,576]{2,1,0:T(2,128)(2,1)S(1)} %copy.31, bf16[16,256,576]{2,1,0:T(8,128)(2,1)} %bitcast.53, f32[16,64]{1,0:T(8,128)S(1)} %fusion.60, f32[16,257,64]{1,2,0:T(8,128)} %copy-done.2), kind=kOutput, calls=%fused_computation.30 | convolution fusion | flops 279220480 | bytes 6842368 | tf_op jit(solution)/shard_map/thp,tpl->thl/dot_general | solution.py:121
  162.7 2.8 %copy.32 = bf16[2,8,64,512]{3,1,2,0:T(8,128)(2,1)} copy(bf16[2,8,64,512]{3,2,1,0:T(8,128)(2,1)} %bitcast.55) | data formatting | bytes 2097152
  165.5 0.6 pad_maximum_fusion
  (34 shorter events, 0.2 us)
Async XLA Ops:
  7.2 103.5 %copy-start = (bf16[32,64,576]{2,1,0:T(8,128)(2,1)S(1)}, bf16[32,64,576]{2,1,0:T(8,128)(2,1)}, u32[]{:S(2)}) copy-start(bf16[32,64,576]{2,1,0:T(8,128)(2,1)} %param.23) | copy-start | bytes 7077892
  7.2 18.7 %copy-start.1 = (bf16[16,3584]{1,0:T(8,128)(2,1)S(1)}, bf16[16,3584]{1,0:T(8,128)(2,1)}, u32[]{:S(2)}) copy-start(bf16[16,3584]{1,0:T(8,128)(2,1)} %param.13) | copy-start | bytes 344068
  7.2 139.9 %all-gather.2.cloned.1.call-start = ((), (), s32[]{:S(2)}) async-start(), calls=%async_computation.3 | async-start | bytes 4659200 | tf_op jit(solution)/shard_map/all_gather | solution.py:95
  14.7 23.5 %all-to-all-start.1 = ((bf16[128,1,2]{2,1,0:T(2,128)(2,1)}), bf16[128,1,2]{2,1,0:T(2,128)(2,1)S(1)}, u32[]{:S(2)}, u32[]{:S(2)}) async-start(bf16[128,1,2]{2,1,0:T(2,128)(2,1)} %all_to_all.16), calls=%async_computation.1 | async-start | bytes 131072 | tf_op jit(solution)/shard_map/all_to_all | solution.py:78
  38.3 37.1 %all-to-all-start = ((bf16[128,2,3584]{2,1,0:T(2,128)(2,1)}), bf16[128,2,3584]{2,1,0:T(2,128)(2,1)}, u32[]{:S(2)}, u32[]{:S(2)}) async-start(bf16[128,2,3584]{2,1,0:T(2,128)(2,1)} %broadcast_select_fusion), calls=%async_computation | async-start | bytes 3670016 | tf_op jit(solution)/shard_map/all_to_all | solution.py:75
  103.8 6.6 %copy-start.6 = (s32[16,4]{0,1:T(4,128)S(1)}, s32[16,4]{0,1:T(4,128)}, u32[]{:S(2)}) copy-start(s32[16,4]{0,1:T(4,128)} %param.24) | copy-start | bytes 772
  103.8 31.6 %all-to-all-start.2 = ((bf16[128,2,3584]{2,1,0:T(2,128)(2,1)}), bf16[128,2,3584]{2,1,0:T(2,128)(2,1)}, u32[]{:S(2)}, u32[]{:S(2)}) async-start(bf16[128,2,3584]{2,1,0:T(2,128)(2,1)} %reshape.134), calls=%async_computation.2 | async-start | bytes 3670016 | tf_op jit(solution)/shard_map/all_to_all | solution.py:86
  110.7 3.5 %copy-start.7 = (s32[1,16]{1,0:T(1,128)S(1)}, s32[1,16]{1,0:T(1,128)}, u32[]{:S(2)}) copy-start(s32[1,16]{1,0:T(1,128)} %param.25) | copy-start | bytes 196
  140.5 6.7 %copy-start.4 = (f32[3584]{0:T(1024)S(1)}, f32[3584]{0:T(1024)}, u32[]{:S(2)}) copy-start(f32[3584]{0:T(1024)} %param.19) | copy-start | bytes 43012
  147.1 3.2 %copy-start.3 = (bf16[16,3584]{1,0:T(8,128)(2,1)}, bf16[16,3584]{1,0:T(8,128)(2,1)S(1)}, u32[]{:S(2)}) copy-start(bf16[16,3584]{1,0:T(8,128)(2,1)S(1)} %get-tuple-element.4) | copy-start | bytes 344068
  147.1 3.3 %copy-start.5 = (f32[512]{0:T(512)S(1)}, f32[512]{0:T(512)}, u32[]{:S(2)}) copy-start(f32[512]{0:T(512)} %param.21) | copy-start | bytes 6148
  147.2 3.5 %copy-start.8 = (bf16[16,64,576]{2,1,0:T(8,128)(2,1)S(1)}, bf16[16,64,576]{2,1,0:T(8,128)(2,1)}, u32[]{:S(2)}) copy-start(bf16[16,64,576]{2,1,0:T(8,128)(2,1)} %param.22) | copy-start | bytes 3538948
  155.3 1.2 copy-start.2
Sparse Core Ops, SparseCore 0:
  10.8 90.1 all-gather.1
where the time goes:
time: 174 us; the launch traced here: 173 us
  waiting for transfers between devices  48.3 us (28%)
  local copies, waits for them, and re-layouts  40.6 us (23%)
  matrix products  32.2 us (19%)
  starting transfers between devices  28.2 us (16%)
  between operations  14.3 us (8%)
  other arithmetic  9.3 us (5%)
    all_to_all x1, waiting for transfers between devices, per_device(): lax.all_to_all(send_rows, ('sec', 'dev'), split_axis=0, concat_axis=0, ti...  26.4 us
    all_to_all x1, waiting for transfers between devices, per_device(): lax.all_to_all(served, ('sec', 'dev'), split_axis=0, concat_axis=0, tiled...  21.2 us
    dot_general x1, matrix products, expert_apply(): result = jnp.dot(hidden, down_proj, preferred_element_type=jnp.float32)  11.6 us
    all_to_all x1, starting transfers between devices, per_device(): lax.all_to_all(send_gate, ('sec', 'dev'), split_axis=0, concat_axis=0, ti...  11.1 us
    all_to_all x1, starting transfers between devices, per_device(): lax.all_to_all(send_rows, ('sec', 'dev'), split_axis=0, concat_axis=0, ti...  10.4 us
    gather x2, local copies, waits for them, and re-layouts, per_device(): tokens[source_row // fanout]  7.73 us
    dot_general x1, matrix products, expert_apply(): gate_part = jnp.dot(rows, gate_proj, preferred_element_type=jnp.float32)  7.05 us
    all_to_all x1, starting transfers between devices, per_device(): lax.all_to_all(served, ('sec', 'dev'), split_axis=0, concat_axis=0, tiled...  6.62 us
  transfers between devices with their start and end apart: 4, of which 2 were waited for; matrix products, arithmetic and copies ran while one was open for 36% of the time, Pallas kernels for 0%

commit v1 on v0

v1 whole, which is shorter than its diff:
```python
import functools

import jax
import jax.numpy as jnp
from jax import lax
from jax.experimental import pallas as pl
from jax.experimental.pallas import tpu as pltpu
from jax.sharding import PartitionSpec as P

MESH = pl.DeviceIdType.MESH
GATE_DEN = 32
CAP = 2
SIDE = 4
score_scale = 192.0 ** (-0.5)
norm_eps = 1e-06
CHUNKS = 4


def rms_scale(values, gain):
    mean_square = jnp.mean(values * values, axis=-1, keepdims=True)
    return values * lax.rsqrt(mean_square + norm_eps) * gain


def place():
    sec, dev = lax.axis_index("sec"), lax.axis_index("dev")
    z = lax.div(dev, SIDE * SIDE)
    x = lax.rem(lax.div(dev, SIDE), SIDE)
    y = lax.rem(dev, SIDE)
    return sec, z, x, y


def partner(here, part, i, back):
    sec, z, x, y = here
    ds, dz, dx = lax.rem(i, 2), lax.rem(lax.div(i, 2), SIDE), lax.div(i, 2 * SIDE)
    dy = lax.rem(part + 2 * SIDE - dz - dx, SIDE)
    if back:
        dz, dx, dy = SIDE - dz, SIDE - dx, SIDE - dy
    return (
        lax.rem(sec + ds, 2),
        lax.rem(z + dz, SIDE) * SIDE * SIDE + lax.rem(x + dx, SIDE) * SIDE + lax.rem(y + dy, SIDE),
    )


def moe_kernel(
    peers,
    tok_ref,
    routes_ref,
    gate_ref,
    w_gate,
    w_up,
    w_down,
    out_ref,
    sent,
    got,
    served,
    back,
    wg,
    wu,
    wd,
    hid,
    rows_buf,
    w_sem,
    sent_sem,
    got_sem,
    served_sem,
    back_sem,
):
    here = place()
    sec, z, x, y = here
    tok_rows, width = tok_ref.shape
    parts = got_sem.shape[0]
    per_part = peers // parts
    quarter = peers // SIDE

    barrier = pltpu.get_barrier_semaphore()

    for q in range(SIDE):

        def greet(i, c, q=q):
            pl.semaphore_signal(barrier, inc=1, device_id=partner(here, q, i, False), device_id_type=MESH)
            return c

        lax.fori_loop(1 if q == 0 else 0, quarter, greet, 0)

    loads = [
        pltpu.make_async_copy(src.at[0], dst, w_sem.at[n])
        for n, (src, dst) in enumerate(((w_gate, wg), (w_up, wu), (w_down, wd)))
    ]
    for load in loads:
        load.start()

    row = lax.broadcasted_iota(jnp.int32, (1, peers * CAP), 1)
    j, c = row >> 1, row & 1
    ds, dz, dx, part = j & 1, (j >> 1) & 3, (j >> 3) & 3, j >> 5
    dy = (part - dz - dx) & 3
    expert = ((sec + ds) & 1) * (peers // 2) + ((z + dz) & 3) * 16 + ((x + dx) & 3) * 4 + ((y + dy) & 3)
    named = jnp.zeros((tok_rows, peers * CAP), jnp.float32)
    gates = jnp.zeros((tok_rows, peers * CAP), jnp.float32)
    for k in range(routes_ref.shape[1]):
        hit = routes_ref[:, k : k + 1] == expert
        named = jnp.where(hit, 1.0, named)
        gates = jnp.where(hit, gate_ref[:, k : k + 1].astype(jnp.float32), gates)
    earlier = (
        lax.broadcasted_iota(jnp.int32, (tok_rows, tok_rows), 1)
        < lax.broadcasted_iota(jnp.int32, (tok_rows, tok_rows), 0)
    ).astype(jnp.float32)
    before = jnp.dot(earlier, named, preferred_element_type=jnp.float32)
    here_slot = before == c.astype(jnp.float32)
    pick = jnp.where(here_slot, named, 0.0).astype(jnp.bfloat16)
    weigh = (jnp.where(here_slot, gates, 0.0) * (1.0 / GATE_DEN)).astype(jnp.bfloat16)

    rows_q = quarter * CAP
    for q in range(SIDE):
        gathered = lax.dot_general(
            pick[:, q * rows_q : (q + 1) * rows_q],
            tok_ref[...],
            (((0,), (0,)), ((), ())),
            preferred_element_type=jnp.float32,
        ).astype(jnp.bfloat16)
        sent[q * quarter : (q + 1) * quarter] = gathered.reshape(quarter, CAP, width)

    pl.semaphore_wait(barrier, peers - 1)

    def exchange(src, dst, src_sem, dst_sem, q, reverse):
        def go(i, c):
            n = q * quarter + i
            pltpu.make_async_remote_copy(
                src_ref=src.at[n],
                dst_ref=dst.at[n],
                send_sem=src_sem,
                recv_sem=dst_sem,
                device_id=partner(here, q, i, reverse),
                device_id_type=MESH,
            ).start()
            return c

        if q == 0:
            pltpu.make_async_copy(src.at[0], dst.at[0], dst_sem).start()
        lax.fori_loop(1 if q == 0 else 0, quarter, go, 0)

    def arrived(dst, sem, lo, n):
        view = dst.at[pl.ds(lo, n)]
        pltpu.make_async_copy(view, view, sem).wait()

    for q in range(SIDE):
        exchange(sent, got, sent_sem, got_sem.at[q * parts // SIDE], q, False)

    for n, load in enumerate(loads):
        load.wait()

    hidden = wg.shape[1]
    tile_h, tile_o = 256, 512
    for p in range(parts):
        arrived(got, got_sem.at[p], p * per_part, per_part)
        rows_buf[...] = got[p * per_part : (p + 1) * per_part].reshape(per_part * CAP, width)

        def up(n, c):
            cols = pl.ds(pl.multiple_of(n * tile_h, tile_h), tile_h)
            g = jnp.dot(rows_buf[...], wg[:, cols], preferred_element_type=jnp.float32)
            u = jnp.dot(rows_buf[...], wu[:, cols], preferred_element_type=jnp.float32)
            hid[:, cols] = (g / (1.0 + jnp.exp(-g)) * u).astype(jnp.bfloat16)
            return c

        lax.fori_loop(0, hidden // tile_h, up, 0)

        def down(n, c, p=p):
            cols = pl.ds(pl.multiple_of(n * tile_o, tile_o), tile_o)
            o = jnp.dot(hid[...], wd[:, cols], preferred_element_type=jnp.float32)
            served[p * per_part : (p + 1) * per_part, :, cols] = o.astype(jnp.bfloat16).reshape(
                per_part, CAP, tile_o
            )
            return c

        lax.fori_loop(0, width // tile_o, down, 0)
        for q in range(p * SIDE // parts, (p + 1) * SIDE // parts):
            exchange(served, back, served_sem, back_sem, q, True)

    arrived(back, back_sem, 0, peers)
    total = tok_ref[...].astype(jnp.float32)
    for q in range(SIDE):
        piece = back[q * quarter : (q + 1) * quarter].reshape(rows_q, width)
        total += jnp.dot(weigh[:, q * rows_q : (q + 1) * rows_q], piece, preferred_element_type=jnp.float32)
    out_ref[...] = total.astype(jnp.bfloat16)

    arrived(sent, sent_sem, 1, peers - 1)
    arrived(served, served_sem, 1, peers - 1)


def moe(tokens, routes, gate_num, w_gate, w_up, w_down, peers):
    tok_rows, width = tokens.shape
    hidden = w_gate.shape[2]
    slots = pltpu.VMEM((peers, CAP, width), jnp.bfloat16)
    rows = peers * CAP // CHUNKS
    dma = pltpu.SemaphoreType.DMA
    return pl.pallas_call(
        functools.partial(moe_kernel, peers),
        out_shape=jax.ShapeDtypeStruct((tok_rows, width), jnp.bfloat16),
        in_specs=[pl.BlockSpec(memory_space=pltpu.VMEM)] * 3 + [pl.BlockSpec(memory_space=pl.ANY)] * 3,
        out_specs=pl.BlockSpec(memory_space=pltpu.VMEM),
        scratch_shapes=[
            slots,
            slots,
            slots,
            slots,
            pltpu.VMEM((width, hidden), jnp.bfloat16),
            pltpu.VMEM((width, hidden), jnp.bfloat16),
            pltpu.VMEM((hidden, width), jnp.bfloat16),
            pltpu.VMEM((rows, hidden), jnp.bfloat16),
            pltpu.VMEM((rows, width), jnp.bfloat16),
            dma((3,)),
            dma,
            dma((CHUNKS,)),
            dma,
            dma,
        ],
        compiler_params=pltpu.CompilerParams(
            collective_id=0, has_side_effects=True, vmem_limit_bytes=56 << 20
        ),
    )(tokens, routes, gate_num, w_gate, w_up, w_down)


def per_device(
    tokens,
    routes,
    gate_num,
    w_gate,
    w_up,
    w_down,
    attn_gain,
    w_latent,
    kv_gain,
    queries,
    cache_pool,
    block_table,
    lengths,
):
    peers = lax.axis_size("sec") * lax.axis_size("dev")
    tok_rows, width = tokens.shape
    layer_out = moe(tokens, routes, gate_num, w_gate, w_up, w_down, peers)
    normed = rms_scale(layer_out.astype(jnp.float32), attn_gain).astype(jnp.bfloat16)
    kdim = w_latent.shape[1]
    lat_width = kv_gain.shape[0]
    latent_full = jnp.dot(
        normed,
        lax.all_gather(w_latent, "dev", axis=0, tiled=True),
        preferred_element_type=jnp.float32,
    )
    latent = rms_scale(latent_full[:, :lat_width], kv_gain)
    new_latent = jnp.concatenate([latent, latent_full[:, lat_width:]], axis=1).astype(jnp.bfloat16)
    page_rows = cache_pool[block_table]
    key_rows = jnp.concatenate(
        [page_rows.reshape(tok_rows, -1, kdim), new_latent[:, None, :]], axis=1
    )
    span = key_rows.shape[1] - 1
    row_lengths = lengths.reshape(-1)
    kept = jnp.concatenate(
        [
            jnp.arange(span, dtype=jnp.int32)[None, :] < row_lengths[:, None],
            jnp.ones((tok_rows, 1), dtype=bool),
        ],
        axis=1,
    )
    scores = (
        jnp.einsum("thk,tpk->thp", queries, key_rows, preferred_element_type=jnp.float32)
        * score_scale
    )
    scores = jnp.where(kept[:, None, :], scores, -1e30)
    top_score = jnp.max(scores, axis=2, keepdims=True)
    raised = jnp.exp(scores - top_score)
    probs = (raised / jnp.sum(raised, axis=2, keepdims=True)).astype(jnp.bfloat16)
    mixed = jnp.einsum(
        "thp,tpl->thl", probs, key_rows[:, :, :lat_width], preferred_element_type=jnp.float32
    )
    context = mixed.astype(jnp.bfloat16).reshape(tok_rows, -1)
    return (layer_out, new_latent, context)


def solution(mesh):
    both = ("sec", "dev")
    return jax.shard_map(
        per_device,
        mesh=mesh,
        in_specs=(
            P(both, None),
            P(both, None),
            P(both, None),
            P(both, None, None),
            P(both, None, None),
            P(both, None, None),
            P(),
            P("dev", None),
            P(),
            P(both, None, None),
            P(both, None, None),
            P(both, None),
            P(both, None),
        ),
        out_specs=(P(both, None), P(both, None), P(both, None)),
        check_vma=False,
    )
```

time: 174 us -> 130 us (0.75)
  Pallas kernels: 0 us -> 58 us
  local copies, waits for them, and re-layouts: 40.6 us -> 11.1 us
  starting transfers between devices: 28.2 us -> 0.04 us
  matrix products: 32.2 us -> 13.4 us
  waiting for transfers between devices: 48.3 us -> 31.1 us
  other arithmetic: 9.3 us -> 2.32 us
    pallas_call x0 -> x1, Pallas kernels: none -> 58 us  [moe(): pl.pallas_call(functools.partial(moe_kernel, peers), out_shape=jax.ShapeD...]
    all_to_all x3 -> x0, waiting for transfers between devices: 47.6 us -> none  [the longest x1 26.4 us: per_device(): lax.all_to_all(send_rows, ('sec', 'dev'), split_axis=0, concat_axis=0, ti...]
    all_gather x1, waiting for transfers between devices: 0.02 us -> 30.4 us  [per_device(): lax.all_gather(w_latent, 'dev', axis=0, tiled=True)]
    all_to_all x3 -> x0, starting transfers between devices: 28.2 us -> none  [the longest x1 11.1 us: per_device(): lax.all_to_all(send_gate, ('sec', 'dev'), split_axis=0, concat_axis=0, ti...]
    dot_general x2 -> x0, matrix products: 18.7 us -> none  [the longest x1 11.6 us: expert_apply(): result = jnp.dot(hidden, down_proj, preferred_element_type=jnp.float32)]
    reshape x4 -> x0, local copies, waits for them, and re-layouts: 14.8 us -> none  [the longest x1 4.97 us: per_device(): picked = returned.reshape(expert_count * capacity, width)[position]]
    gather x4 -> x0, local copies, waits for them, and re-layouts: 14.3 us -> none  [the longest x2 7.73 us: per_device(): tokens[source_row // fanout]]
    select_n x3 -> x0, other arithmetic: 4.5 us -> none  [the longest x1 4.49 us: per_device(): jnp.where(live_slot[:, None], tokens[source_row // fanout], jnp.zeros((),...]
  transfers between devices with their start and end apart: 4 -> 1, of which waited for: 2 -> 1; matrix products, arithmetic and copies ran while one was open for 36% -> 6% of each run, Pallas kernels for 0% -> 45%
where the time goes in v1:
time: 130 us
  Pallas kernels  58 us (45%)
  waiting for transfers between devices  31.1 us (24%)
  between operations  14.2 us (11%)
  matrix products  13.4 us (10%)
  local copies, waits for them, and re-layouts  11.1 us (9%)
  other arithmetic  2.32 us (2%)
    pallas_call x1, Pallas kernels, moe(): pl.pallas_call(functools.partial(moe_kernel, peers), out_shape=jax.ShapeD...  58 us
    all_gather x1, waiting for transfers between devices, per_device(): lax.all_gather(w_latent, 'dev', axis=0, tiled=True)  30.4 us
    unnamed x18, local copies, waits for them, and re-layouts  7.36 us
    dot_general x1, matrix products, per_device(): jnp.einsum('thp,tpl->thl', probs, key_rows[:, :, :lat_width], preferred_e...  5.75 us
    dot_general x1, matrix products, per_device(): jnp.einsum('thk,tpk->thp', queries, key_rows, preferred_element_type=jnp....  4.56 us
    gather x1, local copies, waits for them, and re-layouts, per_device(): page_rows = cache_pool[block_table]  3.49 us
    dot_general x1, matrix products, per_device(): jnp.dot(normed, lax.all_gather(w_latent, 'dev', axis=0, tiled=True), pref...  3.14 us
  transfers between devices with their start and end apart: 1, of which 1 were waited for; matrix products, arithmetic and copies ran while one was open for 6% of the time, Pallas kernels for 45%

profile of v1, /device:TPU:0, one launch (start us, length us, event | category | flops | bytes accessed | tf_op | source)
XLA Modules:
  0.0 130.1 jit_solution(10952235371902661317)
XLA Ops:
  7.2 0.0 copy-start
  7.2 0.0 all-gather.2.cloned.1.call-start
  7.2 0.7 all-gather.2.cloned.1.call-update
  7.9 0.7 compare_select_fusion
  8.6 0.1 copy.22
  8.7 0.1 reshape.69
  8.8 1.4 %copy.20.routes_ref = s32[16,8]{1,0:T(8,128)} copy(s32[16,8]{0,1:T(8,128)} %param.14) | data formatting | bytes 1024 | tf_op args[1]
  10.2 1.4 %copy.21.gate_ref = s32[16,8]{1,0:T(8,128)} copy(s32[16,8]{0,1:T(8,128)} %param.15) | data formatting | bytes 1024 | tf_op args[2]
  11.5 0.0 copy-start.5
  11.5 58.0 %shard_map.148 = bf16[16,3584]{1,0:T(8,128)(2,1)} custom-call(bf16[16,3584]{1,0:T(8,128)(2,1)} %tok_ref.1, s32[16,8]{1,0:T(8,128)} %copy.20.routes_ref, s32[16,8]{1,0:T(8,128)} %copy.21.gate_ref, bf16[1,3584,1024]{2,1,0:T(8,128)(2,1)} %w_gate.1, bf16[1,3584,1024]{2,1,0:T(8,128)(2,1)} %w_up.1, bf16[1,1024,3584]{2,1,0:T(8,128)(2,1)} %w_down.1), custom_call_target="tpu_custom_call" | custom-call | tf_op jit(solution)/shard_map/pallas_call | solution.py:195
  69.5 0.0 copy-done.5
  69.5 0.1 iota_compare_fusion
  69.6 0.0 copy-done
  69.6 0.0 copy-start.1
  69.6 0.0 copy-start.3
  69.7 3.5 %gather_fusion = bf16[64,64,576]{2,1,0:T(8,128)(2,1)} fusion(bf16[32,64,576]{2,1,0:T(8,128)(2,1)S(1)} %copy-done, s32[1024]{0:T(1024)S(1)} %pad_clamp_fusion), kind=kCustom, calls=%fused_computation | custom fusion | bytes 9437440 | tf_op jit(solution)/shard_map/gather | solution.py:250
  73.1 0.0 copy-done.1
  73.1 0.0 copy-start.4
  73.2 0.1 fusion.20
  73.3 30.4 %all-gather.2.cloned.1.call-done = bf16[3584,576]{1,0:T(8,128)(2,1)} async-done(((bf16[56,576]{1,0:T(8,128)(2,1)}), bf16[3584,576]{1,0:T(8,128)(2,1)}) %all-gather.2.cloned.1.call-update) | async-done | bytes 4128784 | tf_op jit(solution)/shard_map/all_gather | solution.py:245
  103.7 0.0 copy-done.3
  103.7 0.0 copy-start.6
  103.7 3.1 %fusion.23 = f32[16,576]{1,0:T(8,128)S(1)} fusion(bf16[3584,576]{1,0:T(8,128)(2,1)} %all-gather.2.cloned.1.call-done, bf16[16,3584]{1,0:T(8,128)(2,1)S(1)} %copy-done.1, f32[3584]{0:T(1024)S(1)} %copy-done.3, f32[16]{0:T(128)S(1)} %add_rsqrt_fusion.1), kind=kOutput, calls=%fused_computation.23 | convolution fusion | flops 66289664 | bytes 4294720 | tf_op jit(solution)/shard_map/dot_general | solution.py:243
  106.9 0.1 multiply_reduce_fusion
  107.0 0.0 copy-done.4
  107.0 0.1 fusion.37
  107.1 0.1 multiply_convert_fusion
  107.2 0.0 copy-done.6
  107.2 4.6 %multiply_select_fusion = f32[16,257,64]{1,2,0:T(8,128)S(1)} fusion(bf16[16,64,576]{2,1,0:T(8,128)(2,1)S(1)} %copy-done.6, bf16[16,1,576]{2,1,0:T(2,128)(2,1)S(1)} %copy.23, bf16[16,256,576]{2,1,0:T(8,128)(2,1)} %bitcast.22, pred[16,257]{1,0:T(8,128)(4,1)S(1)} %concatenate.25), kind=kOutput, calls=%fused_computation.14 | convolution fusion | flops 313169920 | bytes 6973456 | tf_op jit(solution)/shard_map/thk,tpk->thp/dot_general | solution.py:264
  111.8 0.0 copy-start.2
  111.8 1.2 copy-done.2
  113.0 0.5 fusion.34
  113.5 5.8 %fusion.14 = bf16[16,64,512]{2,1,0:T(8,128)(2,1)} fusion(bf16[16,1,576]{2,1,0:T(2,128)(2,1)S(1)} %copy.23, bf16[16,256,576]{2,1,0:T(8,128)(2,1)} %bitcast.23, f32[16,64]{1,0:T(8,128)S(1)} %fusion.34, f32[16,257,64]{1,2,0:T(8,128)} %copy-done.2), kind=kOutput, calls=%fused_computation.16 | convolution fusion | flops 279220480 | bytes 6842368 | tf_op jit(solution)/shard_map/thp,tpl->thl/dot_general | solution.py:271
  119.2 2.8 %copy.24 = bf16[2,8,64,512]{3,1,2,0:T(8,128)(2,1)} copy(bf16[2,8,64,512]{3,2,1,0:T(8,128)(2,1)} %bitcast.25) | data formatting | bytes 2097152
  122.0 0.6 pad_maximum_fusion
  122.6 0.6 copy.26
  (8 shorter events, 0.1 us)
Async XLA Ops:
  7.2 62.5 %copy-start = (bf16[32,64,576]{2,1,0:T(8,128)(2,1)S(1)}, bf16[32,64,576]{2,1,0:T(8,128)(2,1)}, u32[]{:S(2)}) copy-start(bf16[32,64,576]{2,1,0:T(8,128)(2,1)} %param.23) | copy-start | bytes 7077892
  7.2 96.5 %all-gather.2.cloned.1.call-start = ((), (), s32[]{:S(2)}) async-start(), calls=%async_computation | async-start | bytes 4659200 | tf_op jit(solution)/shard_map/all_gather | solution.py:245
  11.5 58.0 %copy-start.5 = (s32[1,16]{1,0:T(1,128)S(1)}, s32[1,16]{1,0:T(1,128)}, u32[]{:S(2)}) copy-start(s32[1,16]{1,0:T(1,128)} %param.25) | copy-start | bytes 196
  69.6 3.5 %copy-start.1 = (bf16[16,3584]{1,0:T(8,128)(2,1)S(1)}, bf16[16,3584]{1,0:T(8,128)(2,1)}, u32[]{:S(2)}) copy-start(bf16[16,3584]{1,0:T(8,128)(2,1)} %shard_map.148) | copy-start | bytes 344068
  69.6 34.1 %copy-start.3 = (f32[3584]{0:T(1024)S(1)}, f32[3584]{0:T(1024)}, u32[]{:S(2)}) copy-start(f32[3584]{0:T(1024)} %param.19) | copy-start | bytes 43012
  73.1 33.9 %copy-start.4 = (f32[512]{0:T(512)S(1)}, f32[512]{0:T(512)}, u32[]{:S(2)}) copy-start(f32[512]{0:T(512)} %param.21) | copy-start | bytes 6148
  103.7 3.5 %copy-start.6 = (bf16[16,64,576]{2,1,0:T(8,128)(2,1)S(1)}, bf16[16,64,576]{2,1,0:T(8,128)(2,1)}, u32[]{:S(2)}) copy-start(bf16[16,64,576]{2,1,0:T(8,128)(2,1)} %param.22) | copy-start | bytes 3538948
  111.8 1.2 copy-start.2
Sparse Core Ops, SparseCore 0:
  10.8 92.8 all-gather.1

commit v2 on v1

v2 whole, which is shorter than its diff:
```python
import functools

import jax
import jax.numpy as jnp
from jax import lax
from jax.experimental import pallas as pl
from jax.experimental.pallas import tpu as pltpu
from jax.sharding import PartitionSpec as P

MESH = pl.DeviceIdType.MESH
GATE_DEN = 32
CAP = 2
SIDE = 4
score_scale = 192.0 ** (-0.5)
norm_eps = 1e-06
CHUNKS = 4
LANE_TILES = 2


def rms_scale(values, gain):
    mean_square = jnp.mean(values * values, axis=-1, keepdims=True)
    return values * lax.rsqrt(mean_square + norm_eps) * gain


def place():
    sec, dev = lax.axis_index("sec"), lax.axis_index("dev")
    z = lax.div(dev, SIDE * SIDE)
    x = lax.rem(lax.div(dev, SIDE), SIDE)
    y = lax.rem(dev, SIDE)
    return sec, z, x, y


def offsets(parts):
    listed = []
    for part in range(parts):
        for i in range(2 * SIDE * SIDE):
            ds, dz, dx = i % 2, i // 2 % SIDE, i // (2 * SIDE)
            listed.append((ds, dz, dx, (part - dz - dx) % SIDE))
    return listed


def finder():
    sec, z, x, y = place()

    def turned(at, size):
        return [at] + [lax.rem(at + step, size) for step in range(1, size)]

    secs, zs, xs, ys = turned(sec, 2), turned(z, SIDE), turned(x, SIDE), turned(y, SIDE)
    planes, lines = [v * (SIDE * SIDE) for v in zs], [v * SIDE for v in xs]

    def find(ds, dz, dx, dy):
        return secs[ds % 2], planes[dz % SIDE] + lines[dx % SIDE] + ys[dy % SIDE]

    return find


def layer_kernel(
    tok_ref,
    routes_ref,
    gate_ref,
    shard_ref,
    attn_gain_ref,
    kv_gain_ref,
    table_ref,
    length_ref,
    w_gate,
    w_up,
    w_down,
    queries,
    pool,
    out_ref,
    latent_ref,
    ctx_ref,
    sent,
    got,
    served,
    back,
    wg,
    wu,
    wd,
    hid,
    rows_buf,
    q_buf,
    pages,
    mixed,
    tops,
    sums,
    fresh,
    wz,
    normed_buf,
    normed_got,
    part_buf,
    part_got,
    load_sem,
    sent_sem,
    got_sem,
    served_sem,
    back_sem,
    wz_sent,
    wz_got,
    swap_sent,
    swap_got,
):
    sec, z, x, y = place()
    find = finder()
    order = offsets(SIDE)
    peers = len(order)
    tok_rows, width = tok_ref.shape
    parts = got_sem.shape[0]
    per_part = peers // parts
    quarter = peers // SIDE
    rows_q = quarter * CAP

    barrier = pltpu.get_barrier_semaphore()
    for offset in order[1:]:
        pl.semaphore_signal(barrier, inc=1, device_id=find(*offset), device_id_type=MESH)

    loads = [
        pltpu.make_async_copy(src, dst, load_sem.at[n])
        for n, (src, dst) in enumerate(
            (
                (queries, q_buf),
                (pool, pages),
                (w_gate.at[0], wg),
                (w_up.at[0], wu),
                (w_down.at[0], wd),
            )
        )
    ]
    for load in loads:
        load.start()

    row = lax.broadcasted_iota(jnp.int32, (1, peers * CAP), 1)
    j, c = row >> 1, row & 1
    ds, dz, dx, part = j & 1, (j >> 1) & 3, (j >> 3) & 3, j >> 5
    dy = (part - dz - dx) & 3
    expert = ((sec + ds) & 1) * (peers // 2) + ((z + dz) & 3) * 16 + ((x + dx) & 3) * 4 + ((y + dy) & 3)
    named = jnp.zeros((tok_rows, peers * CAP), jnp.float32)
    gates = jnp.zeros((tok_rows, peers * CAP), jnp.float32)
    for k in range(routes_ref.shape[1]):
        hit = routes_ref[:, k : k + 1] == expert
        named = jnp.where(hit, 1.0, named)
        gates = jnp.where(hit, gate_ref[:, k : k + 1].astype(jnp.float32), gates)
    earlier = (
        lax.broadcasted_iota(jnp.int32, (tok_rows, tok_rows), 1)
        < lax.broadcasted_iota(jnp.int32, (tok_rows, tok_rows), 0)
    ).astype(jnp.float32)
    before = jnp.dot(earlier, named, preferred_element_type=jnp.float32)
    in_slot = before == c.astype(jnp.float32)
    pick = jnp.where(in_slot, named, 0.0).astype(jnp.bfloat16)
    weigh = (jnp.where(in_slot, gates, 0.0) * (1.0 / GATE_DEN)).astype(jnp.bfloat16)

    for q in range(SIDE):
        gathered = lax.dot_general(
            pick[:, q * rows_q : (q + 1) * rows_q],
            tok_ref[...],
            (((0,), (0,)), ((), ())),
            preferred_element_type=jnp.float32,
        ).astype(jnp.bfloat16)
        sent[q * quarter : (q + 1) * quarter] = gathered.reshape(quarter, CAP, width)
    mine = pl.ds(3 * sec, 2 * LANE_TILES)
    wz[x, y, mine] = shard_ref[mine]

    pl.semaphore_wait(barrier, peers - 1)

    def push(src, dst, src_sem, dst_sem, offset):
        pltpu.make_async_remote_copy(
            src_ref=src,
            dst_ref=dst,
            send_sem=src_sem,
            recv_sem=dst_sem,
            device_id=find(*offset),
            device_id_type=MESH,
        ).start()

    def took(view, sem):
        pltpu.make_async_copy(view, view, sem).wait()

    def exchange(src, dst, src_sem, dst_sem, q, sign):
        for n in range(q * quarter, (q + 1) * quarter):
            if n == 0:
                pltpu.make_async_copy(src.at[0], dst.at[0], dst_sem).start()
            else:
                push(src.at[n], dst.at[n], src_sem, dst_sem, [sign * o for o in order[n]])

    lane_a = pl.ds(3 * sec, LANE_TILES)
    lane_b = pl.ds(3 * sec + LANE_TILES, LANE_TILES)
    other = pl.ds(4 * sec, 3)
    for step in range(1, SIDE):
        view = wz.at[x, y, lane_a]
        push(view, view, wz_sent.at[0], wz_got.at[0], (0, 0, step, 0))
        view = wz.at[x, y, lane_b]
        push(view, view, wz_sent.at[0], wz_got.at[1], (0, 0, 0, step))

    for q in range(2):
        exchange(sent, got, sent_sem, got_sem.at[q * parts // SIDE], q, 1)

    one = wz.at[pl.ds(0, 3), 0, pl.ds(0, LANE_TILES)]
    four = wz.at[pl.ds(0, 3), :, pl.ds(0, LANE_TILES)]
    took(one, wz_got.at[0])
    took(one, wz_got.at[1])
    for step in range(1, SIDE):
        view = wz.at[:, y, lane_a]
        push(view, view, wz_sent.at[1], wz_got.at[2], (0, 0, 0, step))
        view = wz.at[x, :, lane_b]
        push(view, view, wz_sent.at[1], wz_got.at[3], (0, 0, step, 0))

    for q in range(2, SIDE):
        exchange(sent, got, sent_sem, got_sem.at[q * parts // SIDE], q, 1)

    heads, kdim = q_buf.shape[1:]
    lat_width = mixed.shape[2]
    page = pages.shape[1]
    per_row = table_ref.shape[1]
    span = per_row * page
    loads[0].wait()
    loads[1].wait()

    def attend(t, c):
        keys = jnp.concatenate([pages[table_ref[t, i]] for i in range(per_row)], axis=0)
        scores = lax.dot_general(
            q_buf[t], keys, (((1,), (1,)), ((), ())), preferred_element_type=jnp.float32
        )
        kept = lax.broadcasted_iota(jnp.int32, (heads, span), 1) < length_ref[0, t]
        scores = jnp.where(kept, scores * score_scale, -1e30)
        top = jnp.max(scores, axis=1, keepdims=True)
        raised = jnp.where(kept, jnp.exp(scores - top), 0.0)
        tops[t] = top
        sums[t] = jnp.sum(raised, axis=1, keepdims=True)
        mixed[t] = jnp.dot(
            raised.astype(jnp.bfloat16), keys[:, :lat_width], preferred_element_type=jnp.float32
        )
        return c

    lax.fori_loop(0, tok_rows, attend, 0, unroll=2)

    took(four, wz_got.at[2])
    took(four, wz_got.at[3])
    view = wz.at[:, :, other]
    push(view, view, wz_sent.at[2], wz_got.at[4], (1, 0, 0, 0))

    for load in loads[2:]:
        load.wait()

    hidden = wg.shape[1]
    tile_h, tile_o = 256, 512
    for p in range(parts):
        took(got.at[pl.ds(p * per_part, per_part)], got_sem.at[p])
        rows_buf[...] = got[p * per_part : (p + 1) * per_part].reshape(per_part * CAP, width)

        def up(n, c):
            cols = pl.ds(pl.multiple_of(n * tile_h, tile_h), tile_h)
            g = jnp.dot(rows_buf[...], wg[:, cols], preferred_element_type=jnp.float32)
            u = jnp.dot(rows_buf[...], wu[:, cols], preferred_element_type=jnp.float32)
            hid[:, cols] = (g / (1.0 + jnp.exp(-g)) * u).astype(jnp.bfloat16)
            return c

        lax.fori_loop(0, hidden // tile_h, up, 0)

        def down(n, c, p=p):
            cols = pl.ds(pl.multiple_of(n * tile_o, tile_o), tile_o)
            o = jnp.dot(hid[...], wd[:, cols], preferred_element_type=jnp.float32)
            served[p * per_part : (p + 1) * per_part, :, cols] = o.astype(jnp.bfloat16).reshape(
                per_part, CAP, tile_o
            )
            return c

        lax.fori_loop(0, width // tile_o, down, 0)
        for q in range(p * SIDE // parts, (p + 1) * SIDE // parts):
            exchange(served, back, served_sem, back_sem, q, -1)

    took(wz.at[:, :, pl.ds(0, 3)], wz_got.at[4])
    took(back, back_sem)
    total = tok_ref[...].astype(jnp.float32)
    for q in range(SIDE):
        piece = back[q * quarter : (q + 1) * quarter].reshape(rows_q, width)
        total += jnp.dot(weigh[:, q * rows_q : (q + 1) * rows_q], piece, preferred_element_type=jnp.float32)
    layer_out = total.astype(jnp.bfloat16)
    out_ref[...] = layer_out

    normed = rms_scale(layer_out.astype(jnp.float32), attn_gain_ref[...]).astype(jnp.bfloat16)
    share = width // SIDE
    for m in range(SIDE):
        normed_buf[m] = normed[:, m * share : (m + 1) * share]
    zs = [z] + [lax.rem(z + step, SIDE) for step in range(1, SIDE)]
    for step in range(1, SIDE):
        push(normed_buf.at[zs[step]], normed_got.at[z], swap_sent.at[0], swap_got.at[0], (0, step, 0, 0))
    normed_got[z] = normed_buf[z]
    took(normed_got.at[pl.ds(0, SIDE - 1)], swap_got.at[0])
    partial = jnp.dot(
        normed_got[...].reshape(SIDE * tok_rows, share),
        wz[...].reshape(share, kdim),
        preferred_element_type=jnp.float32,
    )
    part_buf[...] = partial.reshape(SIDE, tok_rows, kdim)
    for step in range(1, SIDE):
        push(part_buf.at[zs[step]], part_got.at[z], swap_sent.at[1], swap_got.at[1], (0, step, 0, 0))
    part_got[z] = part_buf[z]
    took(part_got.at[pl.ds(0, SIDE - 1)], swap_got.at[1])
    latent_full = part_got[0] + part_got[1] + part_got[2] + part_got[3]
    latent = rms_scale(latent_full[:, :lat_width], kv_gain_ref[...])
    new_latent = jnp.concatenate([latent, latent_full[:, lat_width:]], axis=1).astype(jnp.bfloat16)
    latent_ref[...] = new_latent

    fresh[...] = lax.dot_general(
        q_buf[...].reshape(tok_rows * heads, kdim),
        new_latent,
        (((1,), (1,)), ((), ())),
        preferred_element_type=jnp.float32,
    ).reshape(tok_rows, heads, tok_rows)

    for t in range(tok_rows):
        score = fresh[t][:, t : t + 1] * score_scale
        top = jnp.maximum(tops[t], score)
        old, new = jnp.exp(tops[t] - top), jnp.exp(score - top)
        scale = 1.0 / (sums[t] * old + new)
        value = new_latent[t : t + 1, :lat_width].astype(jnp.float32)
        ctx_ref[t] = (mixed[t] * (old * scale) + (new * scale) * value).astype(jnp.bfloat16)

    took(sent.at[pl.ds(1, peers - 1)], sent_sem)
    took(served.at[pl.ds(1, peers - 1)], served_sem)
    took(wz.at[pl.ds(0, 3), pl.ds(0, 2), pl.ds(0, LANE_TILES)], wz_sent.at[0])
    took(wz.at[:, pl.ds(0, 3), pl.ds(0, 2 * LANE_TILES)], wz_sent.at[1])
    took(wz.at[:, :, pl.ds(0, 3)], wz_sent.at[2])
    took(normed_buf.at[pl.ds(0, SIDE - 1)], swap_sent.at[0])
    took(part_buf.at[pl.ds(0, SIDE - 1)], swap_sent.at[1])


def per_device(
    tokens,
    routes,
    gate_num,
    w_gate,
    w_up,
    w_down,
    attn_gain,
    w_latent,
    kv_gain,
    queries,
    cache_pool,
    block_table,
    lengths,
):
    peers = lax.axis_size("sec") * lax.axis_size("dev")
    tok_rows, width = tokens.shape
    hidden = w_gate.shape[2]
    heads, kdim = queries.shape[1:]
    lat_width = kv_gain.shape[0]
    tiles = w_latent.shape[0] // 8
    share = width // SIDE
    bf16, f32 = jnp.bfloat16, jnp.float32
    slots = pltpu.VMEM((peers, CAP, width), bf16)
    rows = peers * CAP // CHUNKS
    dma = pltpu.SemaphoreType.DMA
    vmem, smem = pl.BlockSpec(memory_space=pltpu.VMEM), pl.BlockSpec(memory_space=pltpu.SMEM)
    layer_out, new_latent, context = pl.pallas_call(
        layer_kernel,
        out_shape=(
            jax.ShapeDtypeStruct((tok_rows, width), bf16),
            jax.ShapeDtypeStruct((tok_rows, kdim), bf16),
            jax.ShapeDtypeStruct((tok_rows, heads, lat_width), bf16),
        ),
        in_specs=[vmem] * 6 + [smem] * 2 + [pl.BlockSpec(memory_space=pl.ANY)] * 5,
        out_specs=(vmem, vmem, vmem),
        scratch_shapes=[
            slots,
            slots,
            slots,
            slots,
            pltpu.VMEM((width, hidden), bf16),
            pltpu.VMEM((width, hidden), bf16),
            pltpu.VMEM((hidden, width), bf16),
            pltpu.VMEM((rows, hidden), bf16),
            pltpu.VMEM((rows, width), bf16),
            pltpu.VMEM(queries.shape, bf16),
            pltpu.VMEM(cache_pool.shape, bf16),
            pltpu.VMEM((tok_rows, heads, lat_width), f32),
            pltpu.VMEM((tok_rows, heads, 1), f32),
            pltpu.VMEM((tok_rows, heads, 1), f32),
            pltpu.VMEM((tok_rows, heads, tok_rows), f32),
            pltpu.VMEM((SIDE, SIDE, tiles, 8, kdim), bf16),
            pltpu.VMEM((SIDE, tok_rows, share), bf16),
            pltpu.VMEM((SIDE, tok_rows, share), bf16),
            pltpu.VMEM((SIDE, tok_rows, kdim), f32),
            pltpu.VMEM((SIDE, tok_rows, kdim), f32),
            dma((5,)),
            dma,
            dma((CHUNKS,)),
            dma,
            dma,
            dma((3,)),
            dma((5,)),
            dma((2,)),
            dma((2,)),
        ],
        compiler_params=pltpu.CompilerParams(
            collective_id=0, has_side_effects=True, vmem_limit_bytes=60 << 20
        ),
    )(
        tokens,
        routes,
        gate_num,
        w_latent.reshape(tiles, 8, kdim),
        attn_gain[None],
        kv_gain[None],
        block_table,
        lengths,
        w_gate,
        w_up,
        w_down,
        queries,
        cache_pool,
    )
    return (layer_out, new_latent, context.reshape(tok_rows, -1))


def solution(mesh):
    both = ("sec", "dev")
    return jax.shard_map(
        per_device,
        mesh=mesh,
        in_specs=(
            P(both, None),
            P(both, None),
            P(both, None),
            P(both, None, None),
            P(both, None, None),
            P(both, None, None),
            P(),
            P("dev", None),
            P(),
            P(both, None, None),
            P(both, None, None),
            P(both, None),
            P(both, None),
        ),
        out_specs=(P(both, None), P(both, None), P(both, None)),
        check_vma=False,
    )
```

time: 130 us -> 84.4 us (0.65); the launches traced: 130 us -> 82.9 us
  waiting for transfers between devices: 31.1 us -> 0 us
  between operations: 14.2 us -> 0.64 us
  matrix products: 13.4 us -> 0 us
  Pallas kernels: 58 us -> 71.2 us
  other arithmetic: 2.32 us -> 0 us
    all_gather x1 -> x0, waiting for transfers between devices: 30.4 us -> none  [per_device(): lax.all_gather(w_latent, 'dev', axis=0, tiled=True)]
    dot_general x3 -> x0, matrix products: 13.4 us -> none  [the longest x1 5.75 us: per_device(): jnp.einsum('thp,tpl->thl', probs, key_rows[:, :, :lat_width], preferred_e...]
    pallas_call x1, Pallas kernels: 58 us -> 71.2 us  [per_device(): pl.pallas_call(layer_kernel, out_shape=(jax.ShapeDtypeStruct((tok_rows, w...]
    gather x1 -> x0, local copies, waits for them, and re-layouts: 3.49 us -> none  [per_device(): page_rows = cache_pool[block_table]]
    unnamed x18 -> x6, local copies, waits for them, and re-layouts: 7.36 us -> 9.72 us
  transfers between devices with their start and end apart: 1 -> 0, of which waited for: 1 -> 0; matrix products, arithmetic and copies ran while one was open for 6% -> 0% of each run, Pallas kernels for 45% -> 0%
where the time goes in v2:
time: 84.4 us; the launch traced here: 82.9 us
  Pallas kernels  71.2 us (84%)
  local copies, waits for them, and re-layouts  11 us (13%)
    pallas_call x1, Pallas kernels, per_device(): pl.pallas_call(layer_kernel, out_shape=(jax.ShapeDtypeStruct((tok_rows, w...  71.2 us
    unnamed x6, local copies, waits for them, and re-layouts  9.72 us

profile of v2, /device:TPU:0, one launch (start us, length us, event | category | flops | bytes accessed | tf_op | source)
XLA Modules:
  0.0 82.9 jit_solution(14116564745951621461)
XLA Ops:
  0.6 1.4 %copy.16.routes_ref = s32[16,8]{1,0:T(8,128)} copy(s32[16,8]{0,1:T(8,128)} %param.14) | data formatting | bytes 1024 | tf_op args[1]
  2.0 1.4 %copy.17.gate_ref = s32[16,8]{1,0:T(8,128)} copy(s32[16,8]{0,1:T(8,128)} %param.15) | data formatting | bytes 1024 | tf_op args[2]
  3.3 1.4 %copy.18.table_ref = s32[16,4]{1,0:T(8,128)} copy(s32[16,4]{0,1:T(4,128)} %param.24) | data formatting | bytes 512 | tf_op args[11]
  4.7 1.3 %broadcast_in_dim.6.attn_gain_ref = f32[1,3584]{1,0:T(1,128)} reshape(f32[3584]{0:T(1024)} %param.19) | data formatting | bytes 28672 | tf_op jit(solution)/shard_map/broadcast_in_dim | solution.py:404
  6.0 71.2 %shard_map.148 = (bf16[16,3584]{1,0:T(8,128)(2,1)}, bf16[16,576]{1,0:T(8,128)(2,1)}, bf16[16,64,512]{2,1,0:T(8,128)(2,1)}) custom-call(bf16[16,3584]{1,0:T(8,128)(2,1)} %tok_ref.1, s32[16,8]{1,0:T(8,128)} %copy.16.routes_ref, s32[16,8]{1,0:T(8,128)} %copy.17.gate_ref, bf16[7,8,576]{2,1,0:T(8,128)(2,1)} %bitcast.6, f32[1,3584]{1,0:T(1,128)} %broadcast_in_dim.6.attn_gain_ref, ...), custom_call_target="tpu_custom_call" | custom-call | tf_op jit(solution)/shard_map/pallas_call | solution.py:356
  77.3 2.8 %copy.19 = bf16[2,8,64,512]{3,1,2,0:T(8,128)(2,1)} copy(bf16[2,8,64,512]{3,2,1,0:T(8,128)(2,1)} %bitcast.5) | data formatting | bytes 2097152
  80.1 1.6 %copy.22 = bf16[16,3584]{1,0:T(8,128)(2,1)} copy(bf16[16,3584]{1,0:T(8,128)(2,1)} %get-tuple-element.12) | data formatting | bytes 229376
  81.6 1.3 %copy.23 = bf16[16,576]{1,0:T(8,128)(2,1)} copy(bf16[16,576]{1,0:T(8,128)(2,1)} %get-tuple-element.13) | data formatting | bytes 36864

commit v3 on v2

--- a/solution.py
+++ b/solution.py
@@ -37,6 +37,10 @@
             ds, dz, dx = i % 2, i // 2 % SIDE, i // (2 * SIDE)
             listed.append((ds, dz, dx, (part - dz - dx) % SIDE))
     return listed
+
+
+def far_first(numbers, order):
+    return sorted(numbers, key=lambda n: -sum(min(o, SIDE - o) for o in order[n][1:]) if n else 1)
 
 
 def finder():
@@ -85,7 +89,6 @@
     mixed,
     tops,
     sums,
-    fresh,
     wz,
     normed_buf,
     normed_got,
@@ -137,10 +140,12 @@
     expert = ((sec + ds) & 1) * (peers // 2) + ((z + dz) & 3) * 16 + ((x + dx) & 3) * 4 + ((y + dy) & 3)
     named = jnp.zeros((tok_rows, peers * CAP), jnp.float32)
     gates = jnp.zeros((tok_rows, peers * CAP), jnp.float32)
-    for k in range(routes_ref.shape[1]):
-        hit = routes_ref[:, k : k + 1] == expert
+    routes, gate_num = routes_ref[...].astype(jnp.float32).T, gate_ref[...].astype(jnp.float32).T
+    expert = expert.astype(jnp.float32)
+    for k in range(routes.shape[1]):
+        hit = routes[:, k : k + 1] == expert
         named = jnp.where(hit, 1.0, named)
-        gates = jnp.where(hit, gate_ref[:, k : k + 1].astype(jnp.float32), gates)
+        gates = jnp.where(hit, gate_num[:, k : k + 1], gates)
     earlier = (
         lax.broadcasted_iota(jnp.int32, (tok_rows, tok_rows), 1)
         < lax.broadcasted_iota(jnp.int32, (tok_rows, tok_rows), 0)
@@ -177,7 +182,7 @@
         pltpu.make_async_copy(view, view, sem).wait()
 
     def exchange(src, dst, src_sem, dst_sem, q, sign):
-        for n in range(q * quarter, (q + 1) * quarter):
+        for n in far_first(range(q * quarter, (q + 1) * quarter), order):
             if n == 0:
                 pltpu.make_async_copy(src.at[0], dst.at[0], dst_sem).start()
             else:
@@ -211,24 +216,27 @@
     heads, kdim = q_buf.shape[1:]
     lat_width = mixed.shape[2]
     page = pages.shape[1]
-    per_row = table_ref.shape[1]
+    per_row = table_ref.shape[0]
     span = per_row * page
     loads[0].wait()
     loads[1].wait()
 
     def attend(t, c):
-        keys = jnp.concatenate([pages[table_ref[t, i]] for i in range(per_row)], axis=0)
+        keys = jnp.concatenate([pages[table_ref[i, t]] for i in range(per_row)], axis=0)
         scores = lax.dot_general(
-            q_buf[t], keys, (((1,), (1,)), ((), ())), preferred_element_type=jnp.float32
+            keys, q_buf[t], (((1,), (1,)), ((), ())), preferred_element_type=jnp.float32
         )
-        kept = lax.broadcasted_iota(jnp.int32, (heads, span), 1) < length_ref[0, t]
+        kept = lax.broadcasted_iota(jnp.int32, (span, heads), 0) < length_ref[0, t]
         scores = jnp.where(kept, scores * score_scale, -1e30)
-        top = jnp.max(scores, axis=1, keepdims=True)
+        top = jnp.max(scores, axis=0, keepdims=True)
         raised = jnp.where(kept, jnp.exp(scores - top), 0.0)
         tops[t] = top
-        sums[t] = jnp.sum(raised, axis=1, keepdims=True)
-        mixed[t] = jnp.dot(
-            raised.astype(jnp.bfloat16), keys[:, :lat_width], preferred_element_type=jnp.float32
+        sums[t] = jnp.sum(raised, axis=0, keepdims=True)
+        mixed[t] = lax.dot_general(
+            raised.astype(jnp.bfloat16),
+            keys[:, :lat_width],
+            (((0,), (0,)), ((), ())),
+            preferred_element_type=jnp.float32,
         )
         return c
 
@@ -278,7 +286,7 @@
     layer_out = total.astype(jnp.bfloat16)
     out_ref[...] = layer_out
 
-    normed = rms_scale(layer_out.astype(jnp.float32), attn_gain_ref[...]).astype(jnp.bfloat16)
+    normed = rms_scale(layer_out.astype(jnp.float32), attn_gain_ref[...][None]).astype(jnp.bfloat16)
     share = width // SIDE
     for m in range(SIDE):
         normed_buf[m] = normed[:, m * share : (m + 1) * share]
@@ -302,20 +310,25 @@
     new_latent = jnp.concatenate([latent, latent_full[:, lat_width:]], axis=1).astype(jnp.bfloat16)
     latent_ref[...] = new_latent
 
-    fresh[...] = lax.dot_general(
+    against = lax.dot_general(
+        new_latent,
         q_buf[...].reshape(tok_rows * heads, kdim),
-        new_latent,
         (((1,), (1,)), ((), ())),
         preferred_element_type=jnp.float32,
-    ).reshape(tok_rows, heads, tok_rows)
-
-    for t in range(tok_rows):
-        score = fresh[t][:, t : t + 1] * score_scale
-        top = jnp.maximum(tops[t], score)
-        old, new = jnp.exp(tops[t] - top), jnp.exp(score - top)
-        scale = 1.0 / (sums[t] * old + new)
-        value = new_latent[t : t + 1, :lat_width].astype(jnp.float32)
-        ctx_ref[t] = (mixed[t] * (old * scale) + (new * scale) * value).astype(jnp.bfloat16)
+    )
+    own = [against[t : t + 1, t * heads : (t + 1) * heads] for t in range(tok_rows)]
+    score = jnp.concatenate(own, axis=0) * score_scale
+    top_old = jnp.concatenate([tops[t] for t in range(tok_rows)], axis=0)
+    sum_old = jnp.concatenate([sums[t] for t in range(tok_rows)], axis=0)
+    top = jnp.maximum(top_old, score)
+    old, new = jnp.exp(top_old - top), jnp.exp(score - top)
+    scale = 1.0 / (sum_old * old + new)
+    old, new = old * scale, new * scale
+    value = new_latent[:, :lat_width].astype(jnp.float32)
+    for h in range(heads):
+        ctx_ref[:, h * lat_width : (h + 1) * lat_width] = (
+            mixed[:, h, :] * old[:, h : h + 1] + value * new[:, h : h + 1]
+        ).astype(jnp.bfloat16)
 
     took(sent.at[pl.ds(1, peers - 1)], sent_sem)
     took(served.at[pl.ds(1, peers - 1)], served_sem)
@@ -324,6 +337,15 @@
     took(wz.at[:, :, pl.ds(0, 3)], wz_sent.at[2])
     took(normed_buf.at[pl.ds(0, SIDE - 1)], swap_sent.at[0])
     took(part_buf.at[pl.ds(0, SIDE - 1)], swap_sent.at[1])
+
+
+def emit_kernel(a_ref, b_ref, c_ref, a_out, b_out, c_out, sem):
+    pairs = ((a_ref, a_out), (b_ref, b_out), (c_ref, c_out))
+    copies = [pltpu.make_async_copy(src, dst, sem.at[n]) for n, (src, dst) in enumerate(pairs)]
+    for copy in copies:
+        copy.start()
+    for copy in copies:
+        copy.wait()
 
 
 def per_device(
@@ -358,7 +380,7 @@
         out_shape=(
             jax.ShapeDtypeStruct((tok_rows, width), bf16),
             jax.ShapeDtypeStruct((tok_rows, kdim), bf16),
-            jax.ShapeDtypeStruct((tok_rows, heads, lat_width), bf16),
+            jax.ShapeDtypeStruct((tok_rows, heads * lat_width), bf16),
         ),
         in_specs=[vmem] * 6 + [smem] * 2 + [pl.BlockSpec(memory_space=pl.ANY)] * 5,
         out_specs=(vmem, vmem, vmem),
@@ -375,9 +397,8 @@
             pltpu.VMEM(queries.shape, bf16),
             pltpu.VMEM(cache_pool.shape, bf16),
             pltpu.VMEM((tok_rows, heads, lat_width), f32),
-            pltpu.VMEM((tok_rows, heads, 1), f32),
-            pltpu.VMEM((tok_rows, heads, 1), f32),
-            pltpu.VMEM((tok_rows, heads, tok_rows), f32),
+            pltpu.VMEM((tok_rows, 1, heads), f32),
+            pltpu.VMEM((tok_rows, 1, heads), f32),
             pltpu.VMEM((SIDE, SIDE, tiles, 8, kdim), bf16),
             pltpu.VMEM((SIDE, tok_rows, share), bf16),
             pltpu.VMEM((SIDE, tok_rows, share), bf16),
@@ -398,12 +419,12 @@
         ),
     )(
         tokens,
-        routes,
-        gate_num,
+        routes.T,
+        gate_num.T,
         w_latent.reshape(tiles, 8, kdim),
-        attn_gain[None],
+        attn_gain,
         kv_gain[None],
-        block_table,
+        block_table.T,
         lengths,
         w_gate,
         w_up,
@@ -411,7 +432,15 @@
         queries,
         cache_pool,
     )
-    return (layer_out, new_latent, context.reshape(tok_rows, -1))
+    results = (layer_out, new_latent, context)
+    anywhere = pl.BlockSpec(memory_space=pl.ANY)
+    return pl.pallas_call(
+        emit_kernel,
+        out_shape=tuple(jax.ShapeDtypeStruct(v.shape, v.dtype) for v in results),
+        in_specs=[anywhere] * 3,
+        out_specs=(vmem,) * 3,
+        scratch_shapes=[dma((3,))],
+    )(*results)
 
 
 def solution(mesh):

time: 84.4 us -> 73.8 us (0.87); the launches traced: 82.9 us -> 73.6 us
  local copies, waits for them, and re-layouts: 11 us -> 0 us
  Pallas kernels: 71.2 us -> 73 us
    unnamed x6 -> x0, local copies, waits for them, and re-layouts: 9.72 us -> none
    pallas_call x0 -> x1, Pallas kernels: none -> 2.35 us  [per_device(): pl.pallas_call(emit_kernel, out_shape=tuple((jax.ShapeDtypeStruct(v.shape...]
    broadcast_in_dim x1 -> x0, local copies, waits for them, and re-layouts: 1.33 us -> none  [per_device(): attn_gain[None]]
where the time goes in v3:
time: 73.8 us; the launch traced here: 73.6 us
  Pallas kernels  73 us (99%)
    pallas_call x1, Pallas kernels, per_device(): pl.pallas_call(layer_kernel, out_shape=(jax.ShapeDtypeStruct((tok_rows, w...  70.6 us
    pallas_call x1, Pallas kernels, per_device(): pl.pallas_call(emit_kernel, out_shape=tuple((jax.ShapeDtypeStruct(v.shape...  2.35 us

profile of v3, /device:TPU:0, one launch (start us, length us, event | category | flops | bytes accessed | tf_op | source)
XLA Modules:
  0.0 73.6 jit_solution(1428186761790069623)
XLA Ops:
  0.6 70.6 %shard_map.148 = (bf16[16,3584]{1,0:T(8,128)(2,1)}, bf16[16,576]{1,0:T(8,128)(2,1)}, bf16[16,32768]{1,0:T(8,128)(2,1)}) custom-call(bf16[16,3584]{1,0:T(8,128)(2,1)} %tok_ref.1, s32[8,16]{1,0:T(8,128)} %bitcast.6, s32[8,16]{1,0:T(8,128)} %bitcast.7, bf16[7,8,576]{2,1,0:T(8,128)(2,1)} %bitcast.5, f32[3584]{0:T(1024)} %attn_gain_ref.1, f32[1,512]{1,0:T(1,128)} %bitcast.8, ...), custom_call_target="tpu_custom_call" | custom-call | tf_op jit(solution)/shard_map/pallas_call | solution.py:378
  71.3 2.4 %shard_map.149 = (bf16[16,3584]{1,0:T(8,128)(2,1)}, bf16[16,576]{1,0:T(8,128)(2,1)}, bf16[16,32768]{1,0:T(8,128)(2,1)}) custom-call(bf16[16,3584]{1,0:T(8,128)(2,1)} %get-tuple-element.6.a_ref, bf16[16,576]{1,0:T(8,128)(2,1)} %get-tuple-element.7.b_ref, bf16[16,32768]{1,0:T(8,128)(2,1)} %get-tuple-element.8.c_ref), custom_call_target="tpu_custom_call" | custom-call | tf_op jit(solution)/shard_map/pallas_call | solution.py:437

commit v4 on v3

--- a/solution.py
+++ b/solution.py
@@ -32,11 +32,15 @@
 
 def offsets(parts):
     listed = []
-    for part in range(parts):
-        for i in range(2 * SIDE * SIDE):
-            ds, dz, dx = i % 2, i // 2 % SIDE, i // (2 * SIDE)
-            listed.append((ds, dz, dx, (part - dz - dx) % SIDE))
+    for ring in range(2 * SIDE * SIDE):
+        part, ds, dx = ring // (2 * SIDE), ring % 2, ring // 2 % SIDE
+        listed += [(ds, dz, dx, (part - dx) % SIDE) for dz in range(SIDE)]
     return listed
+
+
+def mixed_ways(numbers, order):
+    numbers = list(numbers)
+    return [numbers[(13 * i + 7) % len(numbers)] for i in range(len(numbers))]
 
 
 def far_first(numbers, order):
@@ -58,7 +62,42 @@
     return find
 
 
+def slot_table(routes, gate_num, expert, slot):
+    tok_rows = routes.shape[0]
+    named = jnp.zeros((tok_rows, expert.shape[1]), jnp.float32)
+    gates = jnp.zeros((tok_rows, expert.shape[1]), jnp.float32)
+    for k in range(routes.shape[1]):
+        hit = routes[:, k : k + 1] == expert
+        named = jnp.where(hit, 1.0, named)
+        gates = jnp.where(hit, gate_num[:, k : k + 1], gates)
+    earlier = (
+        lax.broadcasted_iota(jnp.int32, (tok_rows, tok_rows), 1)
+        < lax.broadcasted_iota(jnp.int32, (tok_rows, tok_rows), 0)
+    ).astype(jnp.float32)
+    before = jnp.dot(earlier, named, preferred_element_type=jnp.float32)
+    in_slot = before == slot
+    pick = jnp.where(in_slot, named, 0.0).astype(jnp.bfloat16)
+    weigh = (jnp.where(in_slot, gates, 0.0) * (1.0 / GATE_DEN)).astype(jnp.bfloat16)
+    return pick, weigh
+
+
 def layer_kernel(
+    tok_in,
+    routes_in,
+    gate_in,
+    shard_in,
+    attn_gain_in,
+    kv_gain_in,
+    table_in,
+    length_in,
+    w_gate,
+    w_up,
+    w_down,
+    queries,
+    pool,
+    out_ref,
+    latent_ref,
+    ctx_ref,
     tok_ref,
     routes_ref,
     gate_ref,
@@ -67,14 +106,7 @@
     kv_gain_ref,
     table_ref,
     length_ref,
-    w_gate,
-    w_up,
-    w_down,
-    queries,
-    pool,
-    out_ref,
-    latent_ref,
-    ctx_ref,
+    small_sem,
     sent,
     got,
     served,
@@ -90,8 +122,15 @@
     tops,
     sums,
     wz,
-    normed_buf,
-    normed_got,
+    tok_split,
+    ring_tok,
+    control,
+    ring_control,
+    ring_weigh,
+    gain_split,
+    moe_sum,
+    lo_buf,
+    lo_got,
     part_buf,
     part_got,
     load_sem,
@@ -101,6 +140,8 @@
     back_sem,
     wz_sent,
     wz_got,
+    ring_sent,
+    ring_got,
     swap_sent,
     swap_got,
 ):
@@ -118,6 +159,23 @@
     for offset in order[1:]:
         pl.semaphore_signal(barrier, inc=1, device_id=find(*offset), device_id_type=MESH)
 
+    smalls = [
+        pltpu.make_async_copy(src, dst, small_sem.at[n])
+        for n, (src, dst) in enumerate(
+            (
+                (routes_in, routes_ref),
+                (gate_in, gate_ref),
+                (tok_in, tok_ref),
+                (shard_in, shard_ref),
+                (attn_gain_in, attn_gain_ref),
+                (kv_gain_in, kv_gain_ref),
+                (table_in, table_ref),
+                (length_in, length_ref),
+            )
+        )
+    ]
+    for small in smalls:
+        small.start()
     loads = [
         pltpu.make_async_copy(src, dst, load_sem.at[n])
         for n, (src, dst) in enumerate(
@@ -133,29 +191,18 @@
     for load in loads:
         load.start()
 
+    for small in smalls:
+        small.wait()
+
     row = lax.broadcasted_iota(jnp.int32, (1, peers * CAP), 1)
-    j, c = row >> 1, row & 1
-    ds, dz, dx, part = j & 1, (j >> 1) & 3, (j >> 3) & 3, j >> 5
-    dy = (part - dz - dx) & 3
-    expert = ((sec + ds) & 1) * (peers // 2) + ((z + dz) & 3) * 16 + ((x + dx) & 3) * 4 + ((y + dy) & 3)
-    named = jnp.zeros((tok_rows, peers * CAP), jnp.float32)
-    gates = jnp.zeros((tok_rows, peers * CAP), jnp.float32)
-    routes, gate_num = routes_ref[...].astype(jnp.float32).T, gate_ref[...].astype(jnp.float32).T
-    expert = expert.astype(jnp.float32)
-    for k in range(routes.shape[1]):
-        hit = routes[:, k : k + 1] == expert
-        named = jnp.where(hit, 1.0, named)
-        gates = jnp.where(hit, gate_num[:, k : k + 1], gates)
-    earlier = (
-        lax.broadcasted_iota(jnp.int32, (tok_rows, tok_rows), 1)
-        < lax.broadcasted_iota(jnp.int32, (tok_rows, tok_rows), 0)
-    ).astype(jnp.float32)
-    before = jnp.dot(earlier, named, preferred_element_type=jnp.float32)
-    in_slot = before == c.astype(jnp.float32)
-    pick = jnp.where(in_slot, named, 0.0).astype(jnp.bfloat16)
-    weigh = (jnp.where(in_slot, gates, 0.0) * (1.0 / GATE_DEN)).astype(jnp.bfloat16)
-
-    for q in range(SIDE):
+    slot, dz, ds, dx = (row & 1).astype(jnp.float32), (row >> 1) & 3, (row >> 3) & 1, (row >> 4) & 3
+    dy = ((row >> 6) - dx) & 3
+    in_plane = ((sec + ds) & 1) * (peers // 2) + ((x + dx) & 3) * 4 + ((y + dy) & 3)
+    routes, gate_num = routes_ref[...].astype(jnp.float32), gate_ref[...].astype(jnp.float32)
+    expert = (in_plane + ((z + dz) & 3) * 16).astype(jnp.float32)
+    pick, _ = slot_table(routes.T, gate_num.T, expert, slot)
+
+    def build(q):
         gathered = lax.dot_general(
             pick[:, q * rows_q : (q + 1) * rows_q],
             tok_ref[...],
@@ -163,8 +210,15 @@
             preferred_element_type=jnp.float32,
         ).astype(jnp.bfloat16)
         sent[q * quarter : (q + 1) * quarter] = gathered.reshape(quarter, CAP, width)
+
+    build(0)
     mine = pl.ds(3 * sec, 2 * LANE_TILES)
     wz[x, y, mine] = shard_ref[mine]
+    control[0] = routes
+    control[1] = gate_num
+    share = width // SIDE
+    for m in range(SIDE):
+        tok_split[m] = tok_ref[:, m * share : (m + 1) * share]
 
     pl.semaphore_wait(barrier, peers - 1)
 
@@ -181,12 +235,25 @@
     def took(view, sem):
         pltpu.make_async_copy(view, view, sem).wait()
 
-    def exchange(src, dst, src_sem, dst_sem, q, sign):
+    zs = [z] + [lax.rem(z + step, SIDE) for step in range(1, SIDE)]
+    per_ring = quarter // SIDE
+
+    def dispatch(q):
+        for n in mixed_ways(range(q * quarter, (q + 1) * quarter), order):
+            target = got.at[n // SIDE, z]
+            if n == 0:
+                pltpu.make_async_copy(sent.at[0], target, got_sem.at[0]).start()
+            else:
+                push(sent.at[n], target, sent_sem, got_sem.at[q], order[n])
+
+    def give_back(q):
         for n in far_first(range(q * quarter, (q + 1) * quarter), order):
+            ds, step, dx, dy = order[n]
+            source, target = served.at[zs[step], n // SIDE], back.at[n // SIDE, z]
             if n == 0:
-                pltpu.make_async_copy(src.at[0], dst.at[0], dst_sem).start()
+                pltpu.make_async_copy(source, target, back_sem.at[0]).start()
             else:
-                push(src.at[n], dst.at[n], src_sem, dst_sem, [sign * o for o in order[n]])
+                push(source, target, served_sem, back_sem.at[q], (-ds, step, -dx, -dy))
 
     lane_a = pl.ds(3 * sec, LANE_TILES)
     lane_b = pl.ds(3 * sec + LANE_TILES, LANE_TILES)
@@ -197,9 +264,12 @@
         view = wz.at[x, y, lane_b]
         push(view, view, wz_sent.at[0], wz_got.at[1], (0, 0, 0, step))
 
-    for q in range(2):
-        exchange(sent, got, sent_sem, got_sem.at[q * parts // SIDE], q, 1)
-
+    dispatch(0)
+    for step in range(1, SIDE):
+        push(control, ring_control.at[z], ring_sent.at[0], ring_got.at[0], (0, step, 0, 0))
+        push(tok_split.at[zs[step]], ring_tok.at[z], ring_sent.at[1], ring_got.at[1], (0, step, 0, 0))
+    build(1)
+    dispatch(1)
     one = wz.at[pl.ds(0, 3), 0, pl.ds(0, LANE_TILES)]
     four = wz.at[pl.ds(0, 3), :, pl.ds(0, LANE_TILES)]
     took(one, wz_got.at[0])
@@ -210,8 +280,20 @@
         view = wz.at[x, :, lane_b]
         push(view, view, wz_sent.at[1], wz_got.at[3], (0, 0, step, 0))
 
-    for q in range(2, SIDE):
-        exchange(sent, got, sent_sem, got_sem.at[q * parts // SIDE], q, 1)
+    build(2)
+    dispatch(2)
+    build(3)
+    dispatch(3)
+
+    ring_control[z] = control[...]
+    ring_tok[z] = tok_split[z]
+    gain = attn_gain_ref[...][None]
+    for m in range(SIDE):
+        gain_split[m] = gain[:, m * share : (m + 1) * share]
+    took(ring_control.at[pl.ds(0, SIDE - 1)], ring_got.at[0])
+    expert = (in_plane + dz * 16).astype(jnp.float32)
+    for m in range(SIDE):
+        ring_weigh[m] = slot_table(ring_control[m, 0].T, ring_control[m, 1].T, expert, slot)[1]
 
     heads, kdim = q_buf.shape[1:]
     lat_width = mixed.shape[2]
@@ -240,21 +322,18 @@
         )
         return c
 
-    lax.fori_loop(0, tok_rows, attend, 0, unroll=2)
-
-    took(four, wz_got.at[2])
-    took(four, wz_got.at[3])
-    view = wz.at[:, :, other]
-    push(view, view, wz_sent.at[2], wz_got.at[4], (1, 0, 0, 0))
+    lax.fori_loop(0, 8, attend, 0, unroll=2)
+
 
     for load in loads[2:]:
         load.wait()
 
     hidden = wg.shape[1]
-    tile_h, tile_o = 256, 512
+    tile_h = 256
     for p in range(parts):
-        took(got.at[pl.ds(p * per_part, per_part)], got_sem.at[p])
-        rows_buf[...] = got[p * per_part : (p + 1) * per_part].reshape(per_part * CAP, width)
+        rings = pl.ds(p * per_ring, per_ring)
+        took(got.at[rings], got_sem.at[p])
+        rows_buf[...] = got[rings].reshape(rows_q, width)
 
         def up(n, c):
             cols = pl.ds(pl.multiple_of(n * tile_h, tile_h), tile_h)
@@ -265,47 +344,55 @@
 
         lax.fori_loop(0, hidden // tile_h, up, 0)
 
-        def down(n, c, p=p):
-            cols = pl.ds(pl.multiple_of(n * tile_o, tile_o), tile_o)
+        def down(m, c, rings=rings):
+            cols = pl.ds(pl.multiple_of(m * share, share), share)
             o = jnp.dot(hid[...], wd[:, cols], preferred_element_type=jnp.float32)
-            served[p * per_part : (p + 1) * per_part, :, cols] = o.astype(jnp.bfloat16).reshape(
-                per_part, CAP, tile_o
+            served[m, rings] = o.astype(jnp.bfloat16).reshape(per_ring, SIDE, CAP, share)
+            return c
+
+        lax.fori_loop(0, SIDE, down, 0)
+        give_back(p)
+        if p == 1:
+            took(four, wz_got.at[2])
+            took(four, wz_got.at[3])
+            view = wz.at[:, :, other]
+            push(view, view, wz_sent.at[2], wz_got.at[4], (1, 0, 0, 0))
+        if p == parts - 1:
+            lax.fori_loop(8, 16, attend, 0, unroll=2)
+
+    took(wz.at[:, :, pl.ds(0, 3)], wz_got.at[4])
+    took(ring_tok.at[pl.ds(0, SIDE - 1)], ring_got.at[1])
+
+    for p in range(parts):
+        rings = pl.ds(p * per_ring, per_ring)
+        took(back.at[rings], back_sem.at[p])
+        for m in range(SIDE):
+            piece = back[rings, :, m].reshape(rows_q, share)
+            base = ring_tok[m].astype(jnp.float32) if p == 0 else moe_sum[m]
+            moe_sum[m] = base + jnp.dot(
+                ring_weigh[m, :, p * rows_q : (p + 1) * rows_q], piece, preferred_element_type=jnp.float32
             )
-            return c
-
-        lax.fori_loop(0, width // tile_o, down, 0)
-        for q in range(p * SIDE // parts, (p + 1) * SIDE // parts):
-            exchange(served, back, served_sem, back_sem, q, -1)
-
-    took(wz.at[:, :, pl.ds(0, 3)], wz_got.at[4])
-    took(back, back_sem)
-    total = tok_ref[...].astype(jnp.float32)
-    for q in range(SIDE):
-        piece = back[q * quarter : (q + 1) * quarter].reshape(rows_q, width)
-        total += jnp.dot(weigh[:, q * rows_q : (q + 1) * rows_q], piece, preferred_element_type=jnp.float32)
-    layer_out = total.astype(jnp.bfloat16)
-    out_ref[...] = layer_out
-
-    normed = rms_scale(layer_out.astype(jnp.float32), attn_gain_ref[...][None]).astype(jnp.bfloat16)
-    share = width // SIDE
-    for m in range(SIDE):
-        normed_buf[m] = normed[:, m * share : (m + 1) * share]
-    zs = [z] + [lax.rem(z + step, SIDE) for step in range(1, SIDE)]
-    for step in range(1, SIDE):
-        push(normed_buf.at[zs[step]], normed_got.at[z], swap_sent.at[0], swap_got.at[0], (0, step, 0, 0))
-    normed_got[z] = normed_buf[z]
-    took(normed_got.at[pl.ds(0, SIDE - 1)], swap_got.at[0])
+    layer_out = moe_sum[...].astype(jnp.bfloat16)
+    lo_buf[...] = layer_out
+    wide = layer_out.astype(jnp.float32)
+    squares = jnp.sum(wide * wide, axis=-1, keepdims=True)
+    scaled = (wide * gain_split[z][None]).astype(jnp.bfloat16)
     partial = jnp.dot(
-        normed_got[...].reshape(SIDE * tok_rows, share),
+        scaled.reshape(SIDE * tok_rows, share),
         wz[...].reshape(share, kdim),
         preferred_element_type=jnp.float32,
-    )
-    part_buf[...] = partial.reshape(SIDE, tok_rows, kdim)
+    ).reshape(SIDE, tok_rows, kdim)
+    part_buf[:, :, :kdim] = partial
+    part_buf[:, :, kdim:] = jnp.broadcast_to(squares, (SIDE, tok_rows, part_buf.shape[2] - kdim))
     for step in range(1, SIDE):
         push(part_buf.at[zs[step]], part_got.at[z], swap_sent.at[1], swap_got.at[1], (0, step, 0, 0))
+    for step in range(1, SIDE):
+        push(lo_buf.at[zs[step]], lo_got.at[z], swap_sent.at[0], swap_got.at[0], (0, step, 0, 0))
     part_got[z] = part_buf[z]
+    lo_got[z] = lo_buf[z]
     took(part_got.at[pl.ds(0, SIDE - 1)], swap_got.at[1])
-    latent_full = part_got[0] + part_got[1] + part_got[2] + part_got[3]
+    whole = part_got[0] + part_got[1] + part_got[2] + part_got[3]
+    latent_full = whole[:, :kdim] * lax.rsqrt(whole[:, kdim : kdim + 1] / width + norm_eps)
     latent = rms_scale(latent_full[:, :lat_width], kv_gain_ref[...])
     new_latent = jnp.concatenate([latent, latent_full[:, lat_width:]], axis=1).astype(jnp.bfloat16)
     latent_ref[...] = new_latent
@@ -330,12 +417,19 @@
             mixed[:, h, :] * old[:, h : h + 1] + value * new[:, h : h + 1]
         ).astype(jnp.bfloat16)
 
+    took(lo_got.at[pl.ds(0, SIDE - 1)], swap_got.at[0])
+    for m in range(SIDE):
+        out_ref[:, m * share : (m + 1) * share] = lo_got[m]
+
     took(sent.at[pl.ds(1, peers - 1)], sent_sem)
-    took(served.at[pl.ds(1, peers - 1)], served_sem)
+    took(served.at[pl.ds(0, SIDE - 1)], served_sem)
+    took(served.at[0, pl.ds(1, peers // SIDE - 1)], served_sem)
     took(wz.at[pl.ds(0, 3), pl.ds(0, 2), pl.ds(0, LANE_TILES)], wz_sent.at[0])
     took(wz.at[:, pl.ds(0, 3), pl.ds(0, 2 * LANE_TILES)], wz_sent.at[1])
     took(wz.at[:, :, pl.ds(0, 3)], wz_sent.at[2])
-    took(normed_buf.at[pl.ds(0, SIDE - 1)], swap_sent.at[0])
+    took(ring_control.at[pl.ds(0, SIDE - 1)], ring_sent.at[0])
+    took(tok_split.at[pl.ds(0, SIDE - 1)], ring_sent.at[1])
+    took(lo_buf.at[pl.ds(0, SIDE - 1)], swap_sent.at[0])
     took(part_buf.at[pl.ds(0, SIDE - 1)], swap_sent.at[1])
 
 
@@ -371,7 +465,7 @@
     tiles = w_latent.shape[0] // 8
     share = width // SIDE
     bf16, f32 = jnp.bfloat16, jnp.float32
-    slots = pltpu.VMEM((peers, CAP, width), bf16)
+    rings = peers // SIDE
     rows = peers * CAP // CHUNKS
     dma = pltpu.SemaphoreType.DMA
     vmem, smem = pl.BlockSpec(memory_space=pltpu.VMEM), pl.BlockSpec(memory_space=pltpu.SMEM)
@@ -382,13 +476,22 @@
             jax.ShapeDtypeStruct((tok_rows, kdim), bf16),
             jax.ShapeDtypeStruct((tok_rows, heads * lat_width), bf16),
         ),
-        in_specs=[vmem] * 6 + [smem] * 2 + [pl.BlockSpec(memory_space=pl.ANY)] * 5,
+        in_specs=[pl.BlockSpec(memory_space=pl.ANY)] * 13,
         out_specs=(vmem, vmem, vmem),
         scratch_shapes=[
-            slots,
-            slots,
-            slots,
-            slots,
+            pltpu.VMEM((tok_rows, width), bf16),
+            pltpu.VMEM(routes.shape[::-1], jnp.int32),
+            pltpu.VMEM(gate_num.shape[::-1], jnp.int32),
+            pltpu.VMEM((tiles, 8, kdim), bf16),
+            pltpu.VMEM(attn_gain.shape, f32),
+            pltpu.VMEM((1, lat_width), f32),
+            pltpu.SMEM(block_table.shape[::-1], jnp.int32),
+            pltpu.SMEM(lengths.shape, jnp.int32),
+            dma((8,)),
+            pltpu.VMEM((peers, CAP, width), bf16),
+            pltpu.VMEM((rings, SIDE, CAP, width), bf16),
+            pltpu.VMEM((SIDE, rings, SIDE, CAP, share), bf16),
+            pltpu.VMEM((rings, SIDE, SIDE, CAP, share), bf16),
             pltpu.VMEM((width, hidden), bf16),
             pltpu.VMEM((width, hidden), bf16),
             pltpu.VMEM((hidden, width), bf16),
@@ -402,15 +505,24 @@
             pltpu.VMEM((SIDE, SIDE, tiles, 8, kdim), bf16),
             pltpu.VMEM((SIDE, tok_rows, share), bf16),
             pltpu.VMEM((SIDE, tok_rows, share), bf16),
-            pltpu.VMEM((SIDE, tok_rows, kdim), f32),
-            pltpu.VMEM((SIDE, tok_rows, kdim), f32),
+            pltpu.VMEM((2, routes.shape[1], tok_rows), f32),
+            pltpu.VMEM((SIDE, 2, routes.shape[1], tok_rows), f32),
+            pltpu.VMEM((SIDE, tok_rows, peers * CAP), bf16),
+            pltpu.VMEM((SIDE, 1, share), f32),
+            pltpu.VMEM((SIDE, tok_rows, share), f32),
+            pltpu.VMEM((SIDE, tok_rows, share), bf16),
+            pltpu.VMEM((SIDE, tok_rows, share), bf16),
+            pltpu.VMEM((SIDE, tok_rows, kdim + 64), f32),
+            pltpu.VMEM((SIDE, tok_rows, kdim + 64), f32),
             dma((5,)),
             dma,
             dma((CHUNKS,)),
             dma,
-            dma,
+            dma((CHUNKS,)),
             dma((3,)),
             dma((5,)),
+            dma((2,)),
+            dma((2,)),
             dma((2,)),
             dma((2,)),
         ],

time: 73.8 us -> 69.3 us (0.939)
  Pallas kernels: 73 us -> 68.5 us
    pallas_call x1, Pallas kernels: 70.6 us -> 66.1 us  [per_device(): pl.pallas_call(layer_kernel, out_shape=(jax.ShapeDtypeStruct((tok_rows, w...]
where the time goes in v4:
time: 69.3 us; the launch traced here: 69.1 us
  Pallas kernels  68.5 us (99%)
    pallas_call x1, Pallas kernels, per_device(): pl.pallas_call(layer_kernel, out_shape=(jax.ShapeDtypeStruct((tok_rows, w...  66.1 us
    pallas_call x1, Pallas kernels, per_device(): pl.pallas_call(emit_kernel, out_shape=tuple((jax.ShapeDtypeStruct(v.shape...  2.35 us

profile of v4, /device:TPU:0, one launch (start us, length us, event | category | flops | bytes accessed | tf_op | source)
XLA Modules:
  0.0 69.1 jit_solution(9062968619673800279)
XLA Ops:
  0.6 66.1 %shard_map.148 = (bf16[16,3584]{1,0:T(8,128)(2,1)}, bf16[16,576]{1,0:T(8,128)(2,1)}, bf16[16,32768]{1,0:T(8,128)(2,1)}) custom-call(bf16[16,3584]{1,0:T(8,128)(2,1)} %tok_in.1, s32[8,16]{1,0:T(8,128)} %bitcast.6, s32[8,16]{1,0:T(8,128)} %bitcast.7, bf16[7,8,576]{2,1,0:T(8,128)(2,1)} %bitcast.5, f32[3584]{0:T(1024)} %attn_gain_in.1, f32[1,512]{1,0:T(1,128)} %bitcast.8, ...), custom_call_target="tpu_custom_call" | custom-call | tf_op jit(solution)/shard_map/pallas_call | solution.py:472
  66.8 2.4 %shard_map.149 = (bf16[16,3584]{1,0:T(8,128)(2,1)}, bf16[16,576]{1,0:T(8,128)(2,1)}, bf16[16,32768]{1,0:T(8,128)(2,1)}) custom-call(bf16[16,3584]{1,0:T(8,128)(2,1)} %get-tuple-element.6.a_ref, bf16[16,576]{1,0:T(8,128)(2,1)} %get-tuple-element.7.b_ref, bf16[16,32768]{1,0:T(8,128)(2,1)} %get-tuple-element.8.c_ref), custom_call_target="tpu_custom_call" | custom-call | tf_op jit(solution)/shard_map/pallas_call | solution.py:549

commit v5 on v4

--- a/solution.py
+++ b/solution.py
@@ -97,7 +97,9 @@
     pool,
     out_ref,
     latent_ref,
+    ctx_out,
     ctx_ref,
+    ctx_sem,
     tok_ref,
     routes_ref,
     gate_ref,
@@ -274,14 +276,14 @@
     four = wz.at[pl.ds(0, 3), :, pl.ds(0, LANE_TILES)]
     took(one, wz_got.at[0])
     took(one, wz_got.at[1])
+    build(2)
+    dispatch(2)
     for step in range(1, SIDE):
         view = wz.at[:, y, lane_a]
         push(view, view, wz_sent.at[1], wz_got.at[2], (0, 0, 0, step))
         view = wz.at[x, :, lane_b]
         push(view, view, wz_sent.at[1], wz_got.at[3], (0, 0, step, 0))
 
-    build(2)
-    dispatch(2)
     build(3)
     dispatch(3)
 
@@ -382,8 +384,12 @@
         wz[...].reshape(share, kdim),
         preferred_element_type=jnp.float32,
     ).reshape(SIDE, tok_rows, kdim)
-    part_buf[:, :, :kdim] = partial
-    part_buf[:, :, kdim:] = jnp.broadcast_to(squares, (SIDE, tok_rows, part_buf.shape[2] - kdim))
+    half = (part_buf.shape[2] - kdim) // 2
+    coarse = squares.astype(jnp.bfloat16)
+    fine = (squares - coarse.astype(jnp.float32)).astype(jnp.bfloat16)
+    part_buf[:, :, :kdim] = partial.astype(jnp.bfloat16)
+    part_buf[:, :, kdim : kdim + half] = jnp.broadcast_to(coarse, (SIDE, tok_rows, half))
+    part_buf[:, :, kdim + half :] = jnp.broadcast_to(fine, (SIDE, tok_rows, half))
     for step in range(1, SIDE):
         push(part_buf.at[zs[step]], part_got.at[z], swap_sent.at[1], swap_got.at[1], (0, step, 0, 0))
     for step in range(1, SIDE):
@@ -391,8 +397,9 @@
     part_got[z] = part_buf[z]
     lo_got[z] = lo_buf[z]
     took(part_got.at[pl.ds(0, SIDE - 1)], swap_got.at[1])
-    whole = part_got[0] + part_got[1] + part_got[2] + part_got[3]
-    latent_full = whole[:, :kdim] * lax.rsqrt(whole[:, kdim : kdim + 1] / width + norm_eps)
+    whole = jnp.sum(part_got[...].astype(jnp.float32), axis=0)
+    square_sum = whole[:, kdim : kdim + 1] + whole[:, kdim + half : kdim + half + 1]
+    latent_full = whole[:, :kdim] * lax.rsqrt(square_sum / width + norm_eps)
     latent = rms_scale(latent_full[:, :lat_width], kv_gain_ref[...])
     new_latent = jnp.concatenate([latent, latent_full[:, lat_width:]], axis=1).astype(jnp.bfloat16)
     latent_ref[...] = new_latent
@@ -412,10 +419,16 @@
     scale = 1.0 / (sum_old * old + new)
     old, new = old * scale, new * scale
     value = new_latent[:, :lat_width].astype(jnp.float32)
+    leaving = []
+    batch = heads // ctx_sem.shape[0]
     for h in range(heads):
         ctx_ref[:, h * lat_width : (h + 1) * lat_width] = (
             mixed[:, h, :] * old[:, h : h + 1] + value * new[:, h : h + 1]
         ).astype(jnp.bfloat16)
+        if h % batch == batch - 1:
+            cols = pl.ds((h + 1 - batch) * lat_width, batch * lat_width)
+            leaving.append(pltpu.make_async_copy(ctx_ref.at[:, cols], ctx_out.at[:, cols], ctx_sem.at[h // batch]))
+            leaving[-1].start()
 
     took(lo_got.at[pl.ds(0, SIDE - 1)], swap_got.at[0])
     for m in range(SIDE):
@@ -431,14 +444,25 @@
     took(tok_split.at[pl.ds(0, SIDE - 1)], ring_sent.at[1])
     took(lo_buf.at[pl.ds(0, SIDE - 1)], swap_sent.at[0])
     took(part_buf.at[pl.ds(0, SIDE - 1)], swap_sent.at[1])
-
-
-def emit_kernel(a_ref, b_ref, c_ref, a_out, b_out, c_out, sem):
-    pairs = ((a_ref, a_out), (b_ref, b_out), (c_ref, c_out))
-    copies = [pltpu.make_async_copy(src, dst, sem.at[n]) for n, (src, dst) in enumerate(pairs)]
-    for copy in copies:
+    for copy in leaving:
+        copy.wait()
+
+
+def emit_kernel(a_ref, b_ref, c_ref, a_out, b_out, c_out, a_buf, b_buf, c_buf, in_sem, out_sem):
+    trips = [(a_ref, a_buf, a_out), (b_ref, b_buf, b_out)]
+    pieces = in_sem.shape[0] - len(trips)
+    step = c_ref.shape[1] // pieces
+    for i in range(pieces):
+        cols = pl.ds(i * step, step)
+        trips.append((c_ref.at[:, cols], c_buf.at[:, cols], c_out.at[:, cols]))
+    comes = [pltpu.make_async_copy(src, buf, in_sem.at[n]) for n, (src, buf, _) in enumerate(trips)]
+    goes = [pltpu.make_async_copy(buf, dst, out_sem.at[n]) for n, (_, buf, dst) in enumerate(trips)]
+    for copy in comes:
         copy.start()
-    for copy in copies:
+    for come, go in zip(comes, goes):
+        come.wait()
+        go.start()
+    for copy in goes:
         copy.wait()
 
 
@@ -477,8 +501,10 @@
             jax.ShapeDtypeStruct((tok_rows, heads * lat_width), bf16),
         ),
         in_specs=[pl.BlockSpec(memory_space=pl.ANY)] * 13,
-        out_specs=(vmem, vmem, vmem),
+        out_specs=(vmem, vmem, pl.BlockSpec(memory_space=pl.ANY)),
         scratch_shapes=[
+            pltpu.VMEM((tok_rows, heads * lat_width), bf16),
+            dma((4,)),
             pltpu.VMEM((tok_rows, width), bf16),
             pltpu.VMEM(routes.shape[::-1], jnp.int32),
             pltpu.VMEM(gate_num.shape[::-1], jnp.int32),
@@ -512,8 +538,8 @@
             pltpu.VMEM((SIDE, tok_rows, share), f32),
             pltpu.VMEM((SIDE, tok_rows, share), bf16),
             pltpu.VMEM((SIDE, tok_rows, share), bf16),
-            pltpu.VMEM((SIDE, tok_rows, kdim + 64), f32),
-            pltpu.VMEM((SIDE, tok_rows, kdim + 64), f32),
+            pltpu.VMEM((SIDE, tok_rows, kdim + 64), bf16),
+            pltpu.VMEM((SIDE, tok_rows, kdim + 64), bf16),
             dma((5,)),
             dma,
             dma((CHUNKS,)),
@@ -550,8 +576,8 @@
         emit_kernel,
         out_shape=tuple(jax.ShapeDtypeStruct(v.shape, v.dtype) for v in results),
         in_specs=[anywhere] * 3,
-        out_specs=(vmem,) * 3,
-        scratch_shapes=[dma((3,))],
+        out_specs=(anywhere,) * 3,
+        scratch_shapes=[pltpu.VMEM(v.shape, v.dtype) for v in results] + [dma((6,)), dma((6,))],
     )(*results)
 
 

time: 69.3 us -> 68.4 us (0.987)
  Pallas kernels: 68.5 us -> 67.7 us
where the time goes in v5:
time: 68.4 us; the launch traced here: 68.3 us
  Pallas kernels  67.7 us (99%)
    pallas_call x1, Pallas kernels, per_device(): pl.pallas_call(layer_kernel, out_shape=(jax.ShapeDtypeStruct((tok_rows, w...  65.6 us
    pallas_call x1, Pallas kernels, per_device(): pl.pallas_call(emit_kernel, out_shape=tuple((jax.ShapeDtypeStruct(v.shape...  2.1 us

profile of v5, /device:TPU:0, one launch (start us, length us, event | category | flops | bytes accessed | tf_op | source)
XLA Modules:
  0.0 68.3 jit_solution(6495600455147231088)
XLA Ops:
  0.6 65.6 %shard_map.148 = (bf16[16,3584]{1,0:T(8,128)(2,1)}, bf16[16,576]{1,0:T(8,128)(2,1)}, bf16[16,32768]{1,0:T(8,128)(2,1)}) custom-call(bf16[16,3584]{1,0:T(8,128)(2,1)} %tok_in.1, s32[8,16]{1,0:T(8,128)} %bitcast.6, s32[8,16]{1,0:T(8,128)} %bitcast.7, bf16[7,8,576]{2,1,0:T(8,128)(2,1)} %bitcast.5, f32[3584]{0:T(1024)} %attn_gain_in.1, f32[1,512]{1,0:T(1,128)} %bitcast.8, ...), custom_call_target="tpu_custom_call" | custom-call | tf_op jit(solution)/shard_map/pallas_call | solution.py:496
  66.2 2.1 %shard_map.149 = (bf16[16,3584]{1,0:T(8,128)(2,1)}, bf16[16,576]{1,0:T(8,128)(2,1)}, bf16[16,32768]{1,0:T(8,128)(2,1)}) custom-call(bf16[16,3584]{1,0:T(8,128)(2,1)} %get-tuple-element.6.a_ref, bf16[16,576]{1,0:T(8,128)(2,1)} %get-tuple-element.7.b_ref, bf16[16,32768]{1,0:T(8,128)(2,1)} %get-tuple-element.8.c_ref), custom_call_target="tpu_custom_call" | custom-call | tf_op jit(solution)/shard_map/pallas_call | solution.py:575
